TPU v7x, 128 devices: a whole 4x4x4 slice. The times are simulated.
128 devices in a mesh: seq: 32 (over y_lo, x, z), head: 4 (over y_hi, core).
Axes of the slice: x: 4, y: 4 (y_hi: 2, y_lo: 2; y = y_hi * 2 + y_lo), z: 4, core: 2. Of those that a mesh axis runs over, the one named last changes fastest.
Arguments:
- queries: bfloat16 [16384, 4096], P(('seq', 'head')), may hold values from -8 to 8
- keys: bfloat16 [16384, 2048], P(('seq', 'head')), may hold values from -8 to 8
- values: bfloat16 [16384, 2048], P(('seq', 'head')), may hold values from -6 to 6
- output_cotangent: bfloat16 [16384, 4096], P(('seq', 'head')), may hold values from -6 to 6
Outputs:
- attended: bfloat16 [16384, 4096], P(('seq', 'head'))
- grad_queries: bfloat16 [16384, 4096], P(('seq', 'head'))
- key_gradient: bfloat16 [16384, 2048], P(('seq', 'head'))
- value_gradient: bfloat16 [16384, 2048], P(('seq', 'head'))
All inputs are finite; a program needn't handle non-finite values.
Results may differ from a plain program's by a relative error of at most 0.0095.
Values may be sent and summed in bfloat16 or wider, within the bound.
No kernel may reach another device: no remote copies, remote signals or barrier semaphores. Data moves between devices by JAX's collectives and lax.ppermute only.
A program may use at most 128 MiB of HBM per device.

v0:
```python
import jax
import jax.numpy as jnp
from jax import lax
from jax.sharding import PartitionSpec as P

HEAD_SIZE = 128
WINDOW_TOKENS = 1024


query_scale = 168.0 ** (-0.5)


def passed_along(value, axis, steps):
    count = lax.axis_size(axis)
    leading, last = (max(0, -steps), min(count, count - steps))
    return lax.ppermute(value, axis, [(source, source + steps) for source in range(leading, last)])


def mix(form, left, right):
    return jnp.einsum(form, left, right, preferred_element_type=jnp.float32)


def head_pass(query_head, key_extended, value_extended, grad_head, start, block):
    group_factor, total_count, width = query_head.shape
    steps = total_count // block
    rows = jnp.arange(block, dtype=jnp.int32)[:, None]
    cols = jnp.arange(WINDOW_TOKENS + block, dtype=jnp.int32)[None, :]

    def visit(carry, index):
        dk_acc, dv_acc = carry
        anchor = index * block
        key_pos = start + anchor + cols - WINDOW_TOKENS
        allowed = (cols > rows) & (cols <= rows + WINDOW_TOKENS) & (key_pos >= 0)
        scores = query_scale * mix("rqd,kd->rqk", query_head, key_extended)
        scores = jnp.where(allowed[None], scores, -1e30)
        top = jnp.max(scores, axis=-1, keepdims=True)
        lse = top + jnp.log(jnp.sum(jnp.exp(scores - top), axis=-1, keepdims=True))
        probs = jnp.exp(scores - lse)
        probs_b = probs.astype(jnp.bfloat16)
        out_b = mix("rqk,kd->rqd", probs_b, value_extended).astype(jnp.bfloat16)
        delta = jnp.sum(grad_head.astype(jnp.float32) * out_b.astype(jnp.float32), axis=-1)
        dprobs = mix("rqd,kd->rqk", grad_head, value_extended)
        dscores = (probs * (dprobs - delta[..., None])).astype(jnp.bfloat16)
        dq_b = (query_scale * mix("rqk,kd->rqd", dscores, key_extended)).astype(jnp.bfloat16)
        dk_slab = query_scale * mix("rqk,rqd->kd", dscores, query_head)
        dv_slab = mix("rqk,rqd->kd", probs_b, grad_head)
        dk_acc = dk_acc + dk_slab
        dv_acc = dv_acc + dv_slab
        return ((dk_acc, dv_acc), (out_b, dq_b))

    empty = jnp.zeros((WINDOW_TOKENS + total_count, width), jnp.float32)
    (dk_acc, dv_acc), (outs, grads) = lax.scan(
        visit, (empty, empty), jnp.arange(steps, dtype=jnp.int32)
    )
    outs = outs.transpose(1, 0, 2, 3).reshape(group_factor, total_count, width)
    grads = grads.transpose(1, 0, 2, 3).reshape(group_factor, total_count, width)
    return (outs, grads, dk_acc, dv_acc)


def body(queries, keys, values, output_cotangent):
    length = queries.shape[0] * lax.axis_size("head")
    hops = max(1, WINDOW_TOKENS // length)
    span = min(WINDOW_TOKENS, length)
    q_loc, k_loc, v_loc, g_loc = (
        lax.all_to_all(queries, "head", split_axis=1, concat_axis=0, tiled=True),
        lax.all_to_all(keys, "head", split_axis=1, concat_axis=0, tiled=True),
        lax.all_to_all(values, "head", split_axis=1, concat_axis=0, tiled=True),
        lax.all_to_all(output_cotangent, "head", split_axis=1, concat_axis=0, tiled=True),
    )
    key_parts = []
    value_parts = []
    for hop in range(hops, 0, -1):
        key_far, value_far = passed_along((k_loc, v_loc), "seq", hop)
        key_parts.append(key_far)
        value_parts.append(value_far)
    key_halo = jnp.concatenate(key_parts, 0)
    value_halo = jnp.concatenate(value_parts, 0)
    width = HEAD_SIZE
    groups = k_loc.shape[1] // width
    group_factor = q_loc.shape[1] // width // groups
    start = lax.axis_index("seq") * length
    query_head_rows = q_loc.reshape(length, groups, group_factor, width).transpose(1, 2, 0, 3)
    head_gradients = g_loc.reshape(length, groups, group_factor, width).transpose(1, 2, 0, 3)
    key_extended = (
        jnp.concatenate([key_halo, k_loc], 0)
        .reshape(WINDOW_TOKENS + length, groups, width)
        .transpose(1, 0, 2)
    )
    value_extended = (
        jnp.concatenate([value_halo, v_loc], 0)
        .reshape(WINDOW_TOKENS + length, groups, width)
        .transpose(1, 0, 2)
    )
    block = min(512, length)

    def per_head(parts):
        return head_pass(parts[0], parts[1], parts[2], parts[3], start, block)

    outs, grads_q, key_grad_parts, value_grad_parts = lax.map(
        per_head, (query_head_rows, key_extended, value_extended, head_gradients)
    )
    out_loc = outs.transpose(2, 0, 1, 3).reshape(length, groups * group_factor * width)
    dq_loc = grads_q.transpose(2, 0, 1, 3).reshape(length, groups * group_factor * width)
    dk_ext = key_grad_parts.transpose(1, 0, 2).reshape(WINDOW_TOKENS + length, groups * width)
    dv_ext = value_grad_parts.transpose(1, 0, 2).reshape(WINDOW_TOKENS + length, groups * width)
    tail_k = dk_ext[WINDOW_TOKENS + length - span :]
    tail_v = dv_ext[WINDOW_TOKENS + length - span :]
    for hop in range(1, hops + 1):
        offset = (hops - hop) * span
        back_k, back_v = passed_along(
            (dk_ext[offset : offset + span], dv_ext[offset : offset + span]), "seq", -hop
        )
        tail_k = tail_k + back_k
        tail_v = tail_v + back_v
    dk_loc = jnp.concatenate(
        [dk_ext[WINDOW_TOKENS : WINDOW_TOKENS + length - span], tail_k], 0
    ).astype(jnp.bfloat16)
    dv_loc = jnp.concatenate(
        [dv_ext[WINDOW_TOKENS : WINDOW_TOKENS + length - span], tail_v], 0
    ).astype(jnp.bfloat16)
    attended, grad_queries, key_gradient, value_gradient = (
        lax.all_to_all(out_loc, "head", split_axis=0, concat_axis=1, tiled=True),
        lax.all_to_all(dq_loc, "head", split_axis=0, concat_axis=1, tiled=True),
        lax.all_to_all(dk_loc, "head", split_axis=0, concat_axis=1, tiled=True),
        lax.all_to_all(dv_loc, "head", split_axis=0, concat_axis=1, tiled=True),
    )
    return (attended, grad_queries, key_gradient, value_gradient)


def solution(mesh):
    return jax.shard_map(
        body,
        mesh=mesh,
        in_specs=(
            P(("seq", "head"), None),
            P(("seq", "head"), None),
            P(("seq", "head"), None),
            P(("seq", "head"), None),
        ),
        out_specs=(
            P(("seq", "head"), None),
            P(("seq", "head"), None),
            P(("seq", "head"), None),
            P(("seq", "head"), None),
        ),
        check_vma=False,
    )
```

profile of v0, /device:TPU:14, one launch (start us, length us, event | category | flops | bytes accessed | tf_op | source)
XLA Modules:
  0.0 385.0 jit_solution(2779081421239915388)
XLA Ops:
  2.8 3.6 all-to-all-start.2
  8.5 8.2 %all-to-all-done.2 = bf16[128,4,512]{0,2,1:T(8,128)(2,1)S(1)} async-done(((bf16[128,4,512]{0,2,1:T(8,128)(2,1)}), bf16[128,4,512]{0,2,1:T(8,128)(2,1)S(1)}, u32[]{:S(2)}, u32[]{:S(2)}) %all-to-all-start.2) | async-done | bytes 524320 | tf_op jit(solution)/shard_map/all_to_all | solution.py:67
  17.4 3.5 all-to-all-start.1
  22.2 9.0 %all-to-all-done.1 = bf16[128,4,512]{0,2,1:T(8,128)(2,1)S(1)} async-done(((bf16[128,4,512]{0,2,1:T(8,128)(2,1)}), bf16[128,4,512]{0,2,1:T(8,128)(2,1)S(1)}, u32[]{:S(2)}, u32[]{:S(2)}) %all-to-all-start.1) | async-done | bytes 524320 | tf_op jit(solution)/shard_map/all_to_all | solution.py:66
  31.2 3.5 all-to-all-start.3
  35.8 14.8 %all-to-all-done.3 = bf16[128,4,1024]{0,2,1:T(8,128)(2,1)S(1)} async-done(((bf16[128,4,1024]{0,2,1:T(8,128)(2,1)}), bf16[128,4,1024]{0,2,1:T(8,128)(2,1)S(1)}, u32[]{:S(2)}, u32[]{:S(2)}) %all-to-all-start.3) | async-done | bytes 1048608 | tf_op jit(solution)/shard_map/all_to_all | solution.py:68
  50.6 3.5 all-to-all-start
  55.4 5.8 %collective-permute-start.2 = (bf16[512,512]{1,0:T(8,128)(2,1)S(1)}, bf16[512,512]{1,0:T(8,128)(2,1)}, u32[]{:S(2)}, u32[]{:S(2)}) collective-permute-start(bf16[512,512]{1,0:T(8,128)(2,1)S(1)} %bitcast.154), channel_id=1, source_target_pairs={{0,8},{4,12},{8,16},{12,20},{16,24},{20,28},{24,32},{28,36},{32,40... | collective-permute-start | bytes 1572872 | tf_op jit(solution)/shard_map/ppermute | solution.py:16
  61.2 2.9 collective-permute-start.3
  74.5 2.6 reshape.138
  79.8 17.3 %collective-permute-done.3 = bf16[512,512]{1,0:T(8,128)(2,1)} collective-permute-done((bf16[512,512]{1,0:T(8,128)(2,1)S(1)}, bf16[512,512]{1,0:T(8,128)(2,1)}, u32[]{:S(2)}, u32[]{:S(2)}) %collective-permute-start.3) | collective-permute-done | bytes 524320 | tf_op jit(solution)/shard_map/ppermute | solution.py:16
  98.3 9.1 %maximum_bitcast_fusion.1 = bf16[4,1536,128]{2,0,1:T(4,128)(2,1)S(1)} fusion(bf16[512,4,128]{2,1,0:T(4,128)(2,1)} %concatenate.26, bf16[512,4,128]{2,1,0:T(4,128)(2,1)S(1)} %concatenate.25, bf16[512,4,128]{2,1,0:T(4,128)(2,1)S(1)} %concatenate.24), kind=kLoop, calls=%fused_computation.43 | loop fusion | flops 1572864 | bytes 3145728 | tf_op jit(solution)/shard_map/transpose | solution.py:92
  111.0 8.1 %collective-permute-done.1 = bf16[512,512]{1,0:T(8,128)(2,1)} collective-permute-done((bf16[512,512]{1,0:T(8,128)(2,1)}, bf16[512,512]{1,0:T(8,128)(2,1)}, u32[]{:S(2)}, u32[]{:S(2)}) %collective-permute-start.1) | collective-permute-done | bytes 524320 | tf_op jit(solution)/shard_map/ppermute | solution.py:16
  121.7 108.7 %while.19 = (s32[]{:T(128)}, bf16[4,2,512,128]{2,3,1,0:T(8,128)(2,1)}, bf16[4,2,512,128]{3,2,1,0:T(8,128)(2,1)}, f32[4,1536,128]{1,2,0:T(8,128)}, f32[4,1536,128...) while((s32[]{:T(128)}, ...), condition=%wide.region_4.5_spmd, body=%wide.region_0.4_spmd.sunk | while | flops 2440629248 | bytes 105176296 | solution.py:99
  123.7 2.5 fusion.54
  129.1 5.1 %fusion.57 = f32[4,1536,128]{1,2,0:T(8,128)} fusion(f32[4,1536,128]{1,2,0:T(8,128)} %get-tuple-element.384, s32[]{:T(128)} %get-tuple-element.380, f32[2,512,1536]{2,1,0:T(8,128)} %copy-done, f32[2,512]{1,0:T(2,128)S(1)} %log_add_fusion.2, bf16[1,2,512,128]{2,3,1,0:T(8,128)(2,1)S(1)} %copy.160), kind=kOutput, calls=%fused_computation.10.clone.1 | convolution fusion | flops 405798912 | bytes 7344640 | tf_op jit(solution)/shard_map/while/body/eval_jaxpr/while/body/eval_jaxpr/rqk,rqd->kd/dot_general | solution.py:20
  134.2 3.0 bitcast_dynamic-update-slice_fusion.2
  137.2 2.6 multiply_convert_fusion.2
  146.2 2.7 fusion.55
  156.3 5.1 %fusion.57 = f32[4,1536,128]{1,2,0:T(8,128)} fusion(f32[4,1536,128]{1,2,0:T(8,128)} %get-tuple-element.384, s32[]{:T(128)} %get-tuple-element.380, f32[2,512,1536]{2,1,0:T(8,128)} %copy-done, f32[2,512]{1,0:T(2,128)S(1)} %log_add_fusion.2, bf16[1,2,512,128]{2,3,1,0:T(8,128)(2,1)S(1)} %copy.160), kind=kOutput, calls=%fused_computation.10.clone.1 | convolution fusion | flops 405798912 | bytes 7344640 | tf_op jit(solution)/shard_map/while/body/eval_jaxpr/while/body/eval_jaxpr/rqk,rqd->kd/dot_general | solution.py:20
  161.3 3.0 bitcast_dynamic-update-slice_fusion.2
  164.4 2.6 multiply_convert_fusion.2
  173.3 2.7 fusion.55
  178.1 2.5 fusion.54
  183.4 5.1 %fusion.57 = f32[4,1536,128]{1,2,0:T(8,128)} fusion(f32[4,1536,128]{1,2,0:T(8,128)} %get-tuple-element.384, s32[]{:T(128)} %get-tuple-element.380, f32[2,512,1536]{2,1,0:T(8,128)} %copy-done, f32[2,512]{1,0:T(2,128)S(1)} %log_add_fusion.2, bf16[1,2,512,128]{2,3,1,0:T(8,128)(2,1)S(1)} %copy.160), kind=kOutput, calls=%fused_computation.10.clone.1 | convolution fusion | flops 405798912 | bytes 7344640 | tf_op jit(solution)/shard_map/while/body/eval_jaxpr/while/body/eval_jaxpr/rqk,rqd->kd/dot_general | solution.py:20
  188.5 3.0 bitcast_dynamic-update-slice_fusion.2
  191.6 2.6 multiply_convert_fusion.2
  200.5 2.7 fusion.55
  205.3 2.5 fusion.54
  210.6 5.1 %fusion.57 = f32[4,1536,128]{1,2,0:T(8,128)} fusion(f32[4,1536,128]{1,2,0:T(8,128)} %get-tuple-element.384, s32[]{:T(128)} %get-tuple-element.380, f32[2,512,1536]{2,1,0:T(8,128)} %copy-done, f32[2,512]{1,0:T(2,128)S(1)} %log_add_fusion.2, bf16[1,2,512,128]{2,3,1,0:T(8,128)(2,1)S(1)} %copy.160), kind=kOutput, calls=%fused_computation.10.clone.1 | convolution fusion | flops 405798912 | bytes 7344640 | tf_op jit(solution)/shard_map/while/body/eval_jaxpr/while/body/eval_jaxpr/rqk,rqd->kd/dot_general | solution.py:20
  215.7 3.0 bitcast_dynamic-update-slice_fusion.2
  218.8 2.6 multiply_convert_fusion.2
  227.7 2.7 fusion.55
  233.2 4.4 %all-to-all-start.4 = ((bf16[4,128,1024]{2,1,0:T(8,128)(2,1)}), bf16[4,128,1024]{2,1,0:T(8,128)(2,1)S(1)}, u32[]{:S(2)}, u32[]{:S(2)}) async-start(bf16[4,128,1024]{2,1,0:T(8,128)(2,1)} %copy.137), calls=%async_computation.4 | async-start | bytes 2097152 | tf_op jit(solution)/shard_map/all_to_all | solution.py:122
  237.6 3.7 fusion.30
  246.9 6.8 %collective-permute-start.4 = (f32[512,512]{0,1:T(8,128)}, f32[512,512]{0,1:T(8,128)}, u32[]{:S(2)}, u32[]{:S(2)}) collective-permute-start(f32[512,512]{0,1:T(8,128)} %bitcast.37), channel_id=1, source_target_pairs={{4,0},{8,4},{12,8},{16,12},{20,16},{24,20},{28,24},{32,28},{36,32}... | collective-permute-start | bytes 3145736 | tf_op jit(solution)/shard_map/ppermute | solution.py:16
  258.3 2.7 all-to-all-done.4
  261.0 3.5 all-to-all-start.5
  264.5 24.9 %collective-permute-done.6 = f32[512,512]{0,1:T(8,128)} collective-permute-done((f32[512,512]{0,1:T(8,128)}, f32[512,512]{0,1:T(8,128)}, u32[]{:S(2)}, u32[]{:S(2)}) %collective-permute-start.6) | collective-permute-done | bytes 1048608 | tf_op jit(solution)/shard_map/ppermute | solution.py:16
  289.4 22.5 %collective-permute-done.7 = f32[512,512]{0,1:T(8,128)} collective-permute-done((f32[512,512]{0,1:T(8,128)}, f32[512,512]{0,1:T(8,128)}, u32[]{:S(2)}, u32[]{:S(2)}) %collective-permute-start.7) | collective-permute-done | bytes 1048608 | tf_op jit(solution)/shard_map/ppermute | solution.py:16
  311.8 2.9 fusion.26
  316.8 4.4 %all-to-all-start.7 = ((bf16[4,128,512]{2,1,0:T(8,128)(2,1)}), bf16[4,128,512]{2,1,0:T(8,128)(2,1)}, u32[]{:S(2)}, u32[]{:S(2)}) async-start(bf16[4,128,512]{2,1,0:T(8,128)(2,1)} %bitcast.157), calls=%async_computation.7 | async-start | bytes 1048576 | tf_op jit(solution)/shard_map/all_to_all | solution.py:125
  321.2 13.2 %collective-permute-done.4 = f32[512,512]{0,1:T(8,128)} collective-permute-done((f32[512,512]{0,1:T(8,128)}, f32[512,512]{0,1:T(8,128)}, u32[]{:S(2)}, u32[]{:S(2)}) %collective-permute-start.4) | collective-permute-done | bytes 1048608 | tf_op jit(solution)/shard_map/ppermute | solution.py:16
  334.5 22.3 %collective-permute-done.5 = f32[512,512]{0,1:T(8,128)} collective-permute-done((f32[512,512]{0,1:T(8,128)}, f32[512,512]{0,1:T(8,128)}, u32[]{:S(2)}, u32[]{:S(2)}) %collective-permute-start.5) | collective-permute-done | bytes 1048608 | tf_op jit(solution)/shard_map/ppermute | solution.py:16
  356.7 2.6 fusion.28
  361.4 6.7 %all-to-all-done.7 = bf16[4,128,512]{2,1,0:T(8,128)(2,1)} async-done(((bf16[4,128,512]{2,1,0:T(8,128)(2,1)}), bf16[4,128,512]{2,1,0:T(8,128)(2,1)}, u32[]{:S(2)}, u32[]{:S(2)}) %all-to-all-start.7) | async-done | bytes 524320 | tf_op jit(solution)/shard_map/all_to_all | solution.py:125
  368.1 4.1 %all-to-all-start.6 = ((bf16[4,128,512]{2,1,0:T(8,128)(2,1)}), bf16[4,128,512]{2,1,0:T(8,128)(2,1)}, u32[]{:S(2)}, u32[]{:S(2)}) async-start(bf16[4,128,512]{2,1,0:T(8,128)(2,1)} %bitcast.39), calls=%async_computation.6 | async-start | bytes 1048576 | tf_op jit(solution)/shard_map/all_to_all | solution.py:124
  378.5 4.1 %all-to-all-done.6 = bf16[4,128,512]{2,1,0:T(8,128)(2,1)} async-done(((bf16[4,128,512]{2,1,0:T(8,128)(2,1)}), bf16[4,128,512]{2,1,0:T(8,128)(2,1)}, u32[]{:S(2)}, u32[]{:S(2)}) %all-to-all-start.6) | async-done | bytes 524320 | tf_op jit(solution)/shard_map/all_to_all | solution.py:124
  (134 shorter events, 102.3 us)
Async XLA Ops:
  0.6 20.3 %copy-start.7 = (bf16[128,4096]{1,0:T(8,128)(2,1)S(1)}, bf16[128,4096]{1,0:T(8,128)(2,1)}, u32[]{:S(2)}) copy-start(bf16[128,4096]{1,0:T(8,128)(2,1)} %param.9) | copy-start | bytes 3145732
  2.8 13.9 %all-to-all-start.2 = ((bf16[128,4,512]{0,2,1:T(8,128)(2,1)}), bf16[128,4,512]{0,2,1:T(8,128)(2,1)S(1)}, u32[]{:S(2)}, u32[]{:S(2)}) async-start(bf16[128,4,512]{0,2,1:T(8,128)(2,1)} %bitcast.21), calls=%async_computation.2 | async-start | bytes 1048576 | tf_op jit(solution)/shard_map/all_to_all | solution.py:67
  6.3 28.4 %copy-start.8 = (bf16[128,4096]{1,0:T(8,128)(2,1)S(1)}, bf16[128,4096]{1,0:T(8,128)(2,1)}, u32[]{:S(2)}) copy-start(bf16[128,4096]{1,0:T(8,128)(2,1)} %param.6) | copy-start | bytes 3145732
  16.7 0.8 copy-start.5
  17.4 13.8 %all-to-all-start.1 = ((bf16[128,4,512]{0,2,1:T(8,128)(2,1)}), bf16[128,4,512]{0,2,1:T(8,128)(2,1)S(1)}, u32[]{:S(2)}, u32[]{:S(2)}) async-start(bf16[128,4,512]{0,2,1:T(8,128)(2,1)} %bitcast.15), calls=%async_computation.1 | async-start | bytes 1048576 | tf_op jit(solution)/shard_map/all_to_all | solution.py:66
  31.2 19.4 %all-to-all-start.3 = ((bf16[128,4,1024]{0,2,1:T(8,128)(2,1)}), bf16[128,4,1024]{0,2,1:T(8,128)(2,1)S(1)}, u32[]{:S(2)}, u32[]{:S(2)}) async-start(bf16[128,4,1024]{0,2,1:T(8,128)(2,1)} %bitcast.26), calls=%async_computation.3 | async-start | bytes 2097152 | tf_op jit(solution)/shard_map/all_to_all | solution.py:68
  50.6 26.5 %all-to-all-start = ((bf16[128,4,1024]{2,0,1:T(8,128)(2,1)}), bf16[128,4,1024]{2,0,1:T(8,128)(2,1)S(1)}, u32[]{:S(2)}, u32[]{:S(2)}) async-start(bf16[128,4,1024]{2,0,1:T(8,128)(2,1)} %bitcast.112), calls=%async_computation | async-start | bytes 2097152 | tf_op jit(solution)/shard_map/all_to_all | solution.py:65
  55.4 23.3 %collective-permute-start.2 = (bf16[512,512]{1,0:T(8,128)(2,1)S(1)}, bf16[512,512]{1,0:T(8,128)(2,1)}, u32[]{:S(2)}, u32[]{:S(2)}) collective-permute-start(bf16[512,512]{1,0:T(8,128)(2,1)S(1)} %bitcast.154), channel_id=1, source_target_pairs={{0,8},{4,12},{8,16},{12,20},{16,24},{20,28},{24,32},{28,36},{32,40... | collective-permute-start | bytes 1572872 | tf_op jit(solution)/shard_map/ppermute | solution.py:16
  61.2 35.9 %collective-permute-start.3 = (bf16[512,512]{1,0:T(8,128)(2,1)S(1)}, bf16[512,512]{1,0:T(8,128)(2,1)}, u32[]{:S(2)}, u32[]{:S(2)}) collective-permute-start(bf16[512,512]{1,0:T(8,128)(2,1)S(1)} %bitcast.155), channel_id=1, source_target_pairs={{0,4},{4,8},{8,12},{12,16},{16,20},{20,24},{24,28},{28,32},{32,36}... | collective-permute-start | bytes 1572872 | tf_op jit(solution)/shard_map/ppermute | solution.py:16
  65.2 44.6 %collective-permute-start = (bf16[512,512]{1,0:T(8,128)(2,1)}, bf16[512,512]{1,0:T(8,128)(2,1)}, u32[]{:S(2)}, u32[]{:S(2)}) collective-permute-start(bf16[512,512]{1,0:T(8,128)(2,1)} %bitcast.164), channel_id=1, source_target_pairs={{0,8},{4,12},{8,16},{12,20},{16,24},{20,28},{24,32},{28,36},{32,40... | collective-permute-start | bytes 1572872 | tf_op jit(solution)/shard_map/ppermute | solution.py:16
  67.1 52.0 %collective-permute-start.1 = (bf16[512,512]{1,0:T(8,128)(2,1)}, bf16[512,512]{1,0:T(8,128)(2,1)}, u32[]{:S(2)}, u32[]{:S(2)}) collective-permute-start(bf16[512,512]{1,0:T(8,128)(2,1)} %bitcast.165), channel_id=1, source_target_pairs={{0,4},{4,8},{8,12},{12,16},{16,20},{20,24},{24,28},{28,32},{32,36}... | collective-permute-start | bytes 1572872 | tf_op jit(solution)/shard_map/ppermute | solution.py:16
  107.4 12.9 %copy-start.6 = (bf16[512,4,128]{0,2,1:T(8,128)(2,1)S(1)}, bf16[512,4,128]{0,2,1:T(8,128)(2,1)}, u32[]{:S(2)}) copy-start(bf16[512,4,128]{0,2,1:T(8,128)(2,1)} %reshape.144) | copy-start | bytes 1572868
  123.0 3.2 copy-start.2
  126.3 2.6 copy-start
  129.1 5.1 %copy-start.1 = (f32[2,512,1536]{2,1,0:T(8,128)S(1)}, f32[2,512,1536]{2,1,0:T(8,128)}, u32[]{:S(2)}) copy-start(f32[2,512,1536]{2,1,0:T(8,128)} %copy-done) | copy-start | bytes 18874372 | tf_op jit(solution)/shard_map/while
  137.2 2.6 copy-start.3
  150.2 3.2 copy-start.2
  153.4 2.6 copy-start
  156.2 5.1 %copy-start.1 = (f32[2,512,1536]{2,1,0:T(8,128)S(1)}, f32[2,512,1536]{2,1,0:T(8,128)}, u32[]{:S(2)}) copy-start(f32[2,512,1536]{2,1,0:T(8,128)} %copy-done) | copy-start | bytes 18874372 | tf_op jit(solution)/shard_map/while
  164.4 2.6 copy-start.3
  177.4 3.2 copy-start.2
  180.6 2.6 copy-start
  183.4 5.1 %copy-start.1 = (f32[2,512,1536]{2,1,0:T(8,128)S(1)}, f32[2,512,1536]{2,1,0:T(8,128)}, u32[]{:S(2)}) copy-start(f32[2,512,1536]{2,1,0:T(8,128)} %copy-done) | copy-start | bytes 18874372 | tf_op jit(solution)/shard_map/while
  191.6 2.6 copy-start.3
  204.6 3.2 copy-start.2
  207.8 2.6 copy-start
  210.6 5.1 %copy-start.1 = (f32[2,512,1536]{2,1,0:T(8,128)S(1)}, f32[2,512,1536]{2,1,0:T(8,128)}, u32[]{:S(2)}) copy-start(f32[2,512,1536]{2,1,0:T(8,128)} %copy-done) | copy-start | bytes 18874372 | tf_op jit(solution)/shard_map/while
  218.8 2.6 copy-start.3
  233.2 27.8 %all-to-all-start.4 = ((bf16[4,128,1024]{2,1,0:T(8,128)(2,1)}), bf16[4,128,1024]{2,1,0:T(8,128)(2,1)S(1)}, u32[]{:S(2)}, u32[]{:S(2)}) async-start(bf16[4,128,1024]{2,1,0:T(8,128)(2,1)} %copy.137), calls=%async_computation.4 | async-start | bytes 2097152 | tf_op jit(solution)/shard_map/all_to_all | solution.py:122
  237.6 7.6 %copy-start.4 = (f32[4,1536,128]{1,2,0:T(8,128)S(1)}, f32[4,1536,128]{1,2,0:T(8,128)}, u32[]{:S(2)}) copy-start(f32[4,1536,128]{1,2,0:T(8,128)} %get-tuple-element.200) | copy-start | bytes 9437188
  241.3 48.0 %collective-permute-start.6 = (f32[512,512]{0,1:T(8,128)}, f32[512,512]{0,1:T(8,128)}, u32[]{:S(2)}, u32[]{:S(2)}) collective-permute-start(f32[512,512]{0,1:T(8,128)} %bitcast.44), channel_id=1, source_target_pairs={{4,0},{8,4},{12,8},{16,12},{20,16},{24,20},{28,24},{32,28},{36,32}... | collective-permute-start | bytes 3145736 | tf_op jit(solution)/shard_map/ppermute | solution.py:16
  243.3 68.6 %collective-permute-start.7 = (f32[512,512]{0,1:T(8,128)}, f32[512,512]{0,1:T(8,128)}, u32[]{:S(2)}, u32[]{:S(2)}) collective-permute-start(f32[512,512]{0,1:T(8,128)} %bitcast.45), channel_id=1, source_target_pairs={{8,0},{12,4},{16,8},{20,12},{24,16},{28,20},{32,24},{36,28},{40,32... | collective-permute-start | bytes 3145736 | tf_op jit(solution)/shard_map/ppermute | solution.py:16
  245.2 10.4 %copy-start.9 = (bf16[4,2,512,128]{3,2,1,0:T(8,128)(2,1)S(1)}, bf16[4,2,512,128]{3,2,1,0:T(8,128)(2,1)}, u32[]{:S(2)}) copy-start(bf16[4,2,512,128]{3,2,1,0:T(8,128)(2,1)} %get-tuple-element.199) | copy-start | bytes 3145732
  246.9 87.6 %collective-permute-start.4 = (f32[512,512]{0,1:T(8,128)}, f32[512,512]{0,1:T(8,128)}, u32[]{:S(2)}, u32[]{:S(2)}) collective-permute-start(f32[512,512]{0,1:T(8,128)} %bitcast.37), channel_id=1, source_target_pairs={{4,0},{8,4},{12,8},{16,12},{20,16},{24,20},{28,24},{32,28},{36,32}... | collective-permute-start | bytes 3145736 | tf_op jit(solution)/shard_map/ppermute | solution.py:16
  253.7 103.0 %collective-permute-start.5 = (f32[512,512]{0,1:T(8,128)}, f32[512,512]{0,1:T(8,128)}, u32[]{:S(2)}, u32[]{:S(2)}) collective-permute-start(f32[512,512]{0,1:T(8,128)} %bitcast.38), channel_id=1, source_target_pairs={{8,0},{12,4},{16,8},{20,12},{24,16},{28,20},{32,24},{36,28},{40,32... | collective-permute-start | bytes 3145736 | tf_op jit(solution)/shard_map/ppermute | solution.py:16
  261.0 55.8 %all-to-all-start.5 = ((bf16[4,128,1024]{2,1,0:T(8,128)(2,1)}), bf16[4,128,1024]{2,1,0:T(8,128)(2,1)S(1)}, u32[]{:S(2)}, u32[]{:S(2)}) async-start(bf16[4,128,1024]{2,1,0:T(8,128)(2,1)} %all_to_all.126), calls=%async_computation.5 | async-start | bytes 2097152 | tf_op jit(solution)/shard_map/all_to_all | solution.py:123
  316.8 51.3 %all-to-all-start.7 = ((bf16[4,128,512]{2,1,0:T(8,128)(2,1)}), bf16[4,128,512]{2,1,0:T(8,128)(2,1)}, u32[]{:S(2)}, u32[]{:S(2)}) async-start(bf16[4,128,512]{2,1,0:T(8,128)(2,1)} %bitcast.157), calls=%async_computation.7 | async-start | bytes 1048576 | tf_op jit(solution)/shard_map/all_to_all | solution.py:125
  368.1 14.5 %all-to-all-start.6 = ((bf16[4,128,512]{2,1,0:T(8,128)(2,1)}), bf16[4,128,512]{2,1,0:T(8,128)(2,1)}, u32[]{:S(2)}, u32[]{:S(2)}) async-start(bf16[4,128,512]{2,1,0:T(8,128)(2,1)} %bitcast.39), calls=%async_computation.6 | async-start | bytes 1048576 | tf_op jit(solution)/shard_map/all_to_all | solution.py:124
where the time goes:
time: 387 us; the launch traced here: 385 us
  waiting for transfers between devices  154 us (40%)
  local copies, waits for them, and re-layouts  80.2 us (21%)
  matrix products  71 us (18%)
  starting transfers between devices  55.7 us (14%)
  other arithmetic  23.1 us (6%)
    ppermute x8, waiting for transfers between devices, passed_along(): lax.ppermute(value, axis, [(source, source + steps) for source in range(l...  108 us
    dot_general x24, matrix products, mix(): return jnp.einsum(form, left, right, preferred_element_type=jnp.float32)  71 us
    ppermute x8, starting transfers between devices, passed_along(): lax.ppermute(value, axis, [(source, source + steps) for source in range(l...  25.1 us
    dynamic_update_slice x8, local copies, waits for them, and re-layouts, body(): lax.map(per_head, (query_head_rows, key_extended, value_extended, head_gr...  17.6 us
    all_to_all x1, waiting for transfers between devices, body(): lax.all_to_all(output_cotangent, 'head', split_axis=1, concat_axis=0, til...  14.8 us
    unnamed x19, local copies, waits for them, and re-layouts  11 us
    transpose x1, other arithmetic, body(): value_extended = jnp.concatenate([value_halo, v_loc], 0).reshape(WINDOW_T...  9.13 us
    all_to_all x1, waiting for transfers between devices, body(): lax.all_to_all(keys, 'head', split_axis=1, concat_axis=0, tiled=True)  8.97 us
  transfers between devices with their start and end apart: 16, of which 12 were waited for; matrix products, arithmetic and copies ran while one was open for 14% of the time, Pallas kernels for 0%

commit v1 on v0

v1 whole, which is shorter than its diff:
```python
import functools

import jax
import jax.numpy as jnp
from jax import lax
from jax.experimental import pallas as pl
from jax.experimental.pallas import tpu as pltpu
from jax.sharding import Mesh, PartitionSpec as P

D = 128
WINDOW = 1024
BLOCK = 256
CHUNKS = WINDOW // BLOCK
SCALE = 168.0 ** (-0.5)
LOG2E = 1.4426950408889634
NEG = -1e30


def cost(flops, bytes_accessed, transcendentals=0):
    return pl.CostEstimate(flops=int(flops), bytes_accessed=int(bytes_accessed), transcendentals=int(transcendentals))


def pack(arrays, widths, heads, step=4):
    rows = arrays[0].shape[0]
    total = sum(widths)

    def kernel(*refs):
        out = refs[-1]
        for j in range(step):
            at = 0
            for ref, w in zip(refs[:-1], widths):
                out[j, :, at : at + w] = ref[:, j * w : (j + 1) * w]
                at += w

    return pl.pallas_call(
        kernel,
        grid=(heads // step,),
        in_specs=[pl.BlockSpec((rows, step * w), lambda i: (0, i)) for w in widths],
        out_specs=pl.BlockSpec((step, rows, total), lambda i: (i, 0, 0)),
        out_shape=jax.ShapeDtypeStruct((heads, rows, total), arrays[0].dtype),
        cost_estimate=cost(0, 4 * heads * rows * total),
        name="pack",
    )(*arrays)


def unpack(packed, widths, step=4):
    heads, rows, total = packed.shape

    def kernel(*refs):
        src = refs[0]
        for j in range(step):
            at = 0
            for ref, w in zip(refs[1:], widths):
                ref[:, j * w : (j + 1) * w] = src[j, :, at : at + w]
                at += w

    return pl.pallas_call(
        kernel,
        grid=(heads // step,),
        in_specs=[pl.BlockSpec((step, rows, total), lambda i: (i, 0, 0))],
        out_specs=[pl.BlockSpec((rows, step * w), lambda i: (0, i)) for w in widths],
        out_shape=[jax.ShapeDtypeStruct((rows, heads * w), packed.dtype) for w in widths],
        cost_estimate=cost(0, 4 * heads * rows * total),
        name="unpack",
    )(packed)


def dot(a, b, ca, cb):
    return lax.dot_general(a, b, (((ca,), (cb,)), ((), ())), preferred_element_type=jnp.float32)


def attention_kernel(factor, first_ref, qg_ref, kv_ref, halo_ref, od_ref, dkv_ref, back_ref, kx, acc_k, acc_v, sems):
    tokens = qg_ref.shape[0]
    own = pltpu.make_async_copy(kv_ref, kx.at[pl.ds(WINDOW, tokens)], sems.at[0])
    halo = pltpu.make_async_copy(halo_ref, kx.at[pl.ds(0, WINDOW)], sems.at[1])
    own.start()
    halo.start()
    acc_k[...] = jnp.zeros_like(acc_k)
    acc_v[...] = jnp.zeros_like(acc_v)
    own.wait()
    halo.wait()
    first = first_ref[0]
    span = WINDOW + BLOCK
    row = lax.broadcasted_iota(jnp.int32, (BLOCK, BLOCK), 0)
    col = lax.broadcasted_iota(jnp.int32, (BLOCK, BLOCK), 1)
    old = col > row

    @pl.loop(0, tokens // BLOCK)
    def _(b):
        r0 = pl.multiple_of(b * BLOCK, BLOCK)
        keys = kx[pl.ds(r0, span), 0:D]
        values = kx[pl.ds(r0, span), D : 2 * D]
        hide = [jnp.where((first == 1) & (b + c < CHUNKS), 1e30, 0.0).astype(jnp.float32) for c in range(CHUNKS)]
        probs_all, ds_all, q_all, g_all = [], [], [], []
        for h in range(factor):
            q = qg_ref[pl.ds(r0, BLOCK), h * D : (h + 1) * D]
            g = qg_ref[pl.ds(r0, BLOCK), (factor + h) * D : (factor + h + 1) * D]
            s = dot(q, keys, 1, 1)
            parts = [jnp.where(old, s[:, 0:BLOCK] - hide[0], s[:, WINDOW:span])]
            parts += [s[:, c * BLOCK : (c + 1) * BLOCK] for c in range(1, CHUNKS)]
            top = jnp.max(parts[0], axis=-1, keepdims=True)
            for c in range(1, CHUNKS):
                top = jnp.maximum(top, jnp.max(parts[c], axis=-1, keepdims=True) - hide[c])
            top = top * (SCALE * LOG2E)
            es = [jnp.exp2(parts[0] * (SCALE * LOG2E) - top)]
            es += [jnp.exp2(parts[c] * (SCALE * LOG2E) - (top + hide[c])) for c in range(1, CHUNKS)]
            norm = jnp.sum(es[0] + es[1] + es[2] + es[3], axis=-1, keepdims=True)
            inv = 1.0 / norm
            ps = [e * inv for e in es]
            pb0 = ps[0].astype(jnp.bfloat16)
            zero = jnp.zeros_like(pb0)
            pb = jnp.concatenate(
                [jnp.where(old, pb0, zero)] + [p.astype(jnp.bfloat16) for p in ps[1:]] + [jnp.where(old, zero, pb0)], axis=1
            )
            out = dot(pb, values, 1, 0).astype(jnp.bfloat16)
            delta = jnp.sum(g.astype(jnp.float32) * out.astype(jnp.float32), axis=-1, keepdims=True)
            dp = dot(g, values, 1, 1)
            dparts = [jnp.where(old, dp[:, 0:BLOCK], dp[:, WINDOW:span])]
            dparts += [dp[:, c * BLOCK : (c + 1) * BLOCK] for c in range(1, CHUNKS)]
            dss = [(p * (x - delta)).astype(jnp.bfloat16) for p, x in zip(ps, dparts)]
            ds = jnp.concatenate([jnp.where(old, dss[0], zero)] + dss[1:] + [jnp.where(old, zero, dss[0])], axis=1)
            od_ref[pl.ds(r0, BLOCK), h * D : (h + 1) * D] = out
            dq = dot(ds, keys, 1, 0) * SCALE
            od_ref[pl.ds(r0, BLOCK), (factor + h) * D : (factor + h + 1) * D] = dq.astype(jnp.bfloat16)
            probs_all.append(pb)
            ds_all.append(ds)
            q_all.append(q)
            g_all.append(g)
        dk = dot(jnp.concatenate(ds_all, 0), jnp.concatenate(q_all, 0), 0, 0)
        dv = dot(jnp.concatenate(probs_all, 0), jnp.concatenate(g_all, 0), 0, 0)
        acc_k[pl.ds(r0, span), :] += dk
        acc_v[pl.ds(r0, span), :] += dv

    dkv_ref[:, 0:D] = acc_k[WINDOW:, :] * SCALE
    dkv_ref[:, D : 2 * D] = acc_v[WINDOW:, :]
    back_ref[:, 0:D] = (acc_k[:WINDOW, :] * SCALE).astype(back_ref.dtype)
    back_ref[:, D : 2 * D] = acc_v[:WINDOW, :].astype(back_ref.dtype)


def attention(first, qg, kv, halo):
    tokens = qg.shape[0]
    factor = qg.shape[1] // (2 * D)
    vmem = pl.BlockSpec(memory_space=pltpu.VMEM)
    pairs = factor * tokens * (WINDOW + BLOCK)
    return pl.pallas_call(
        functools.partial(attention_kernel, factor),
        in_specs=[pl.BlockSpec(memory_space=pltpu.SMEM), vmem, pl.BlockSpec(memory_space=pl.ANY), pl.BlockSpec(memory_space=pl.ANY)],
        out_specs=[vmem, vmem, vmem],
        out_shape=[
            jax.ShapeDtypeStruct((tokens, 2 * factor * D), jnp.bfloat16),
            jax.ShapeDtypeStruct((tokens, 2 * D), jnp.float32),
            jax.ShapeDtypeStruct((WINDOW, 2 * D), jnp.bfloat16),
        ],
        scratch_shapes=[
            pltpu.VMEM((WINDOW + tokens, 2 * D), jnp.bfloat16),
            pltpu.VMEM((WINDOW + tokens, D), jnp.float32),
            pltpu.VMEM((WINDOW + tokens, D), jnp.float32),
            pltpu.SemaphoreType.DMA((2,)),
        ],
        compiler_params=pltpu.CompilerParams(vmem_limit_bytes=56 * 1024 * 1024),
        cost_estimate=cost(12 * pairs * D, 12e6, pairs),
        name="attention",
    )(first, qg, kv, halo)


def body(queries, keys, values, output_cotangent):
    axes = ("row", "head")
    heads = lax.axis_size("row") * lax.axis_size("head")
    rows = queries.shape[0]
    wide = queries.shape[1] // heads
    slim = keys.shape[1] // heads
    groups = lax.axis_size("group")
    first = (lax.axis_index("group") == 0).astype(jnp.int32).reshape(1)

    def spread(x):
        return lax.all_to_all(x, axes, split_axis=0, concat_axis=0, tiled=True)

    kv = spread(pack([keys, values], [slim, slim], heads)).reshape(heads * rows, 2 * slim)
    halo = lax.ppermute(kv[heads * rows - WINDOW :], "group", [(i, i + 1) for i in range(groups - 1)])
    qg = spread(pack([queries, output_cotangent], [wide, wide], heads)).reshape(heads * rows, 2 * wide)
    od, dkv, back = attention(first, qg, kv, halo)
    more = lax.ppermute(back, "group", [(i + 1, i) for i in range(groups - 1)])
    od = spread(od.reshape(heads, rows, 2 * wide))
    tail = heads * rows - WINDOW
    dkv = jnp.concatenate([dkv[:tail], dkv[tail:] + more.astype(jnp.float32)], 0).astype(jnp.bfloat16)
    dkv = spread(dkv.reshape(heads, rows, 2 * slim))
    attended, grad_queries = unpack(od, [wide, wide])
    key_gradient, value_gradient = unpack(dkv, [slim, slim])
    return attended, grad_queries, key_gradient, value_gradient


def solution(mesh):
    row = 4
    seq, head = mesh.devices.shape
    finer = Mesh(mesh.devices.reshape(seq // row, row, head), ("group", "row", "head"))
    spec = P(("group", "row", "head"), None)
    return jax.shard_map(body, mesh=finer, in_specs=(spec,) * 4, out_specs=(spec,) * 4, check_vma=False)
```

time: 387 us -> 183 us (0.47)
  the two profiles are of different devices: /device:TPU:14 before, /device:TPU:1 now
where the time goes in v1:
time: 183 us; the launch traced here: 182 us
  waiting for transfers between devices  86 us (47%)
  Pallas kernels  44.3 us (24%)
  starting transfers between devices  23.2 us (13%)
  blocking collectives  21.8 us (12%)
  local copies, waits for them, and re-layouts  4.77 us (3%)
    all_to_all x3, waiting for transfers between devices, spread(): return lax.all_to_all(x, axes, split_axis=0, concat_axis=0, tiled=True)  62.7 us
    pallas_call x1, Pallas kernels, attention(): pl.pallas_call(functools.partial(attention_kernel, factor), in_specs=[pl....  29.8 us
    all_to_all x1, blocking collectives, spread(): return lax.all_to_all(x, axes, split_axis=0, concat_axis=0, tiled=True)  21.8 us
    all_to_all x3, starting transfers between devices, spread(): return lax.all_to_all(x, axes, split_axis=0, concat_axis=0, tiled=True)  18.7 us
    ppermute x1, waiting for transfers between devices, body(): more = lax.ppermute(back, 'group', [(i + 1, i) for i in range(groups - 1)])  12 us
    ppermute x1, waiting for transfers between devices, body(): lax.ppermute(kv[heads * rows - WINDOW:], 'group', [(i, i + 1) for i in ra...  11.3 us
    pallas_call x2, Pallas kernels, unpack(): pl.pallas_call(kernel, grid=(heads // step,), in_specs=[pl.BlockSpec((ste...  7.24 us
    pallas_call x2, Pallas kernels, pack(): pl.pallas_call(kernel, grid=(heads // step,), in_specs=[pl.BlockSpec((row...  7.23 us
  transfers between devices with their start and end apart: 5, of which 5 were waited for; matrix products, arithmetic and copies ran while one was open for 1% of the time, Pallas kernels for 4%

profile of v1, /device:TPU:1, one launch (start us, length us, event | category | flops | bytes accessed | tf_op | source)
XLA Modules:
  0.0 182.2 jit_solution(6999401709202419461)
XLA Ops:
  0.6 3.5 %pack.3 = bf16[16,128,256]{2,1,0:T(8,128)(2,1)} custom-call(bf16[128,2048]{1,0:T(8,128)(2,1)} %refs_0_.3, bf16[128,2048]{1,0:T(8,128)(2,1)} %refs_1_.3), custom_call_target="tpu_custom_call" | custom-call | bytes 2097152 | tf_op jit(solution)/shard_map/pack/pallas_call | solution.py:35
  4.1 9.4 %all-to-all-start.1 = ((bf16[16,128,256]{2,1,0:T(8,128)(2,1)}), bf16[16,128,256]{2,1,0:T(8,128)(2,1)S(1)}, u32[]{:S(2)}, u32[]{:S(2)}) async-start(bf16[16,128,256]{2,1,0:T(8,128)(2,1)} %pack.3), calls=%async_computation.1 | async-start | bytes 2097152 | tf_op jit(solution)/shard_map/all_to_all | solution.py:176
  13.6 3.8 %pack.2 = bf16[16,128,512]{2,1,0:T(8,128)(2,1)} custom-call(bf16[128,4096]{1,0:T(8,128)(2,1)} %refs_0_.2, bf16[128,4096]{1,0:T(8,128)(2,1)} %refs_1_.2), custom_call_target="tpu_custom_call" | custom-call | bytes 4194304 | tf_op jit(solution)/shard_map/pack/pallas_call | solution.py:35
  17.3 13.3 %all-to-all-done.1 = bf16[16,128,256]{2,1,0:T(8,128)(2,1)S(1)} async-done(((bf16[16,128,256]{2,1,0:T(8,128)(2,1)}), bf16[16,128,256]{2,1,0:T(8,128)(2,1)S(1)}, u32[]{:S(2)}, u32[]{:S(2)}) %all-to-all-start.1) | async-done | bytes 1048608 | tf_op jit(solution)/shard_map/all_to_all | solution.py:176
  30.6 0.0 copy-start.1
  30.6 4.5 %all-to-all-start = ((bf16[16,128,512]{2,1,0:T(8,128)(2,1)}), bf16[16,128,512]{2,1,0:T(8,128)(2,1)S(1)}, u32[]{:S(2)}, u32[]{:S(2)}) async-start(bf16[16,128,512]{2,1,0:T(8,128)(2,1)} %pack.2), calls=%async_computation | async-start | bytes 4194304 | tf_op jit(solution)/shard_map/all_to_all | solution.py:176
  35.2 0.8 slice.17
  36.0 0.0 copy-done.1
  36.0 3.1 %collective-permute-start = (bf16[1024,256]{1,0:T(8,128)(2,1)}, bf16[1024,256]{1,0:T(8,128)(2,1)S(1)}, u32[]{:S(2)}, u32[]{:S(2)}) collective-permute-start(bf16[1024,256]{1,0:T(8,128)(2,1)} %bitcast.3), channel_id=1, source_target_pairs={{0,16},{16,32},{32,48},{48,64},{64,80},{80,96},{96,112},{1,17},{17... | collective-permute-start | bytes 1572872 | tf_op jit(solution)/shard_map/ppermute | solution.py:179
  39.1 11.3 %collective-permute-done.halo_ref = bf16[1024,256]{1,0:T(8,128)(2,1)S(1)} collective-permute-done((bf16[1024,256]{1,0:T(8,128)(2,1)}, bf16[1024,256]{1,0:T(8,128)(2,1)S(1)}, u32[]{:S(2)}, u32[]{:S(2)}) %collective-permute-start) | collective-permute-done | bytes 524320 | tf_op jit(solution)/shard_map/ppermute | solution.py:179
  50.5 0.0 copy-start.3
  50.5 24.3 %all-to-all-done = bf16[16,128,512]{2,1,0:T(8,128)(2,1)S(1)} async-done(((bf16[16,128,512]{2,1,0:T(8,128)(2,1)}), bf16[16,128,512]{2,1,0:T(8,128)(2,1)S(1)}, u32[]{:S(2)}, u32[]{:S(2)}) %all-to-all-start) | async-done | bytes 2097184 | tf_op jit(solution)/shard_map/all_to_all | solution.py:176
  74.8 0.0 copy-start.2
  74.8 0.0 copy-done.3
  74.8 1.3 copy-done.2
  76.1 29.8 %attention.1 = (bf16[2048,512]{1,0:T(8,128)(2,1)}, f32[2048,256]{1,0:T(8,128)}, bf16[1024,256]{1,0:T(8,128)(2,1)}) custom-call(s32[1]{0:T(128)} %bitcast.first_ref, bf16[2048,512]{1,0:T(8,128)(2,1)} %bitcast.8, bf16[2048,256]{1,0:T(8,128)(2,1)} %bitcast.7, bf16[1024,256]{1,0:T(8,128)(2,1)} %copy-done.3), custom_call_target="tpu_custom_call" | custom-call | flops 8053063680 | bytes 12000000 | tf_op jit(solution)/shard_map/attention/pallas_call | solution.py:145
  105.9 1.3 collective-permute-start.1
  107.2 1.3 slice.21
  108.5 12.0 %collective-permute-done.1 = bf16[1024,256]{1,0:T(8,128)(2,1)S(1)} collective-permute-done((bf16[1024,256]{1,0:T(8,128)(2,1)}, bf16[1024,256]{1,0:T(8,128)(2,1)S(1)}, u32[]{:S(2)}, u32[]{:S(2)}) %collective-permute-start.1) | collective-permute-done | bytes 524320 | tf_op jit(solution)/shard_map/ppermute | solution.py:182
  120.6 1.3 add_convert_fusion
  121.9 0.1 pad_maximum_fusion
  122.0 21.8 %all_to_all.20.refs_0_ = bf16[16,128,256]{2,1,0:T(8,128)(2,1)} all-to-all(bf16[16,128,256]{2,1,0:T(8,128)(2,1)S(1)} %bitcast.6), channel_id=1, replica_groups=mesh['group'=8,'row'=4,'head'=4] {'row','head'}, dimensions={0} | all-to-all | bytes 2097152 | tf_op jit(solution)/shard_map/all_to_all | solution.py:176
  143.8 4.8 %all-to-all-start.2 = ((bf16[16,128,512]{2,1,0:T(8,128)(2,1)}), bf16[16,128,512]{2,1,0:T(8,128)(2,1)S(1)}, u32[]{:S(2)}, u32[]{:S(2)}) async-start(bf16[16,128,512]{2,1,0:T(8,128)(2,1)} %bitcast.9), calls=%async_computation.2 | async-start | bytes 4194304 | tf_op jit(solution)/shard_map/all_to_all | solution.py:176
  148.6 3.4 %unpack.3 = (bf16[128,2048]{1,0:T(8,128)(2,1)}, bf16[128,2048]{1,0:T(8,128)(2,1)}) custom-call(bf16[16,128,256]{2,1,0:T(8,128)(2,1)} %all_to_all.20.refs_0_), custom_call_target="tpu_custom_call" | custom-call | bytes 2097152 | tf_op jit(solution)/shard_map/unpack/pallas_call | solution.py:57
  152.0 25.0 %all-to-all-done.2.refs_0_ = bf16[16,128,512]{2,1,0:T(8,128)(2,1)S(1)} async-done(((bf16[16,128,512]{2,1,0:T(8,128)(2,1)}), bf16[16,128,512]{2,1,0:T(8,128)(2,1)S(1)}, u32[]{:S(2)}, u32[]{:S(2)}) %all-to-all-start.2) | async-done | bytes 2097184 | tf_op jit(solution)/shard_map/all_to_all | solution.py:176
  177.0 0.0 copy-start
  177.0 1.3 copy-done
  178.3 3.8 %unpack.2 = (bf16[128,4096]{1,0:T(8,128)(2,1)}, bf16[128,4096]{1,0:T(8,128)(2,1)}) custom-call(bf16[16,128,512]{2,1,0:T(8,128)(2,1)} %copy-done), custom_call_target="tpu_custom_call" | custom-call | bytes 4194304 | tf_op jit(solution)/shard_map/unpack/pallas_call | solution.py:57
Async XLA Ops:
  4.1 26.5 %all-to-all-start.1 = ((bf16[16,128,256]{2,1,0:T(8,128)(2,1)}), bf16[16,128,256]{2,1,0:T(8,128)(2,1)S(1)}, u32[]{:S(2)}, u32[]{:S(2)}) async-start(bf16[16,128,256]{2,1,0:T(8,128)(2,1)} %pack.3), calls=%async_computation.1 | async-start | bytes 2097152 | tf_op jit(solution)/shard_map/all_to_all | solution.py:176
  30.6 5.4 %copy-start.1 = (bf16[16,128,256]{2,1,0:T(8,128)(2,1)}, bf16[16,128,256]{2,1,0:T(8,128)(2,1)S(1)}, u32[]{:S(2)}) copy-start(bf16[16,128,256]{2,1,0:T(8,128)(2,1)S(1)} %all-to-all-done.1) | copy-start | bytes 3145732
  30.6 44.2 %all-to-all-start = ((bf16[16,128,512]{2,1,0:T(8,128)(2,1)}), bf16[16,128,512]{2,1,0:T(8,128)(2,1)S(1)}, u32[]{:S(2)}, u32[]{:S(2)}) async-start(bf16[16,128,512]{2,1,0:T(8,128)(2,1)} %pack.2), calls=%async_computation | async-start | bytes 4194304 | tf_op jit(solution)/shard_map/all_to_all | solution.py:176
  36.0 14.5 %collective-permute-start = (bf16[1024,256]{1,0:T(8,128)(2,1)}, bf16[1024,256]{1,0:T(8,128)(2,1)S(1)}, u32[]{:S(2)}, u32[]{:S(2)}) collective-permute-start(bf16[1024,256]{1,0:T(8,128)(2,1)} %bitcast.3), channel_id=1, source_target_pairs={{0,16},{16,32},{32,48},{48,64},{64,80},{80,96},{96,112},{1,17},{17... | collective-permute-start | bytes 1572872 | tf_op jit(solution)/shard_map/ppermute | solution.py:179
  50.5 24.3 %copy-start.3 = (bf16[1024,256]{1,0:T(8,128)(2,1)}, bf16[1024,256]{1,0:T(8,128)(2,1)S(1)}, u32[]{:S(2)}) copy-start(bf16[1024,256]{1,0:T(8,128)(2,1)S(1)} %collective-permute-done.halo_ref) | copy-start | bytes 1572868
  74.8 1.3 copy-start.2
  105.9 14.6 %collective-permute-start.1 = (bf16[1024,256]{1,0:T(8,128)(2,1)}, bf16[1024,256]{1,0:T(8,128)(2,1)S(1)}, u32[]{:S(2)}, u32[]{:S(2)}) collective-permute-start(bf16[1024,256]{1,0:T(8,128)(2,1)} %get-tuple-element.15), channel_id=1, source_target_pairs={{16,0},{32,16},{48,32},{64,48},{80,64},{96,80},{112,96},{17,1},{33... | collective-permute-start | bytes 1572872 | tf_op jit(solution)/shard_map/ppermute | solution.py:182
  143.8 33.2 %all-to-all-start.2 = ((bf16[16,128,512]{2,1,0:T(8,128)(2,1)}), bf16[16,128,512]{2,1,0:T(8,128)(2,1)S(1)}, u32[]{:S(2)}, u32[]{:S(2)}) async-start(bf16[16,128,512]{2,1,0:T(8,128)(2,1)} %bitcast.9), calls=%async_computation.2 | async-start | bytes 4194304 | tf_op jit(solution)/shard_map/all_to_all | solution.py:176
  177.0 1.3 copy-start

commit v2 on v1

v2 whole, which is shorter than its diff:
```python
import functools

import jax
import jax.numpy as jnp
from jax import lax
from jax.experimental import pallas as pl
from jax.experimental.pallas import tpu as pltpu
from jax.sharding import Mesh, PartitionSpec as P

D = 128
WINDOW = 1024
BLOCK = 256
CHUNKS = WINDOW // BLOCK
SPAN = WINDOW + BLOCK
SCALE = 168.0 ** (-0.5)
RATE = SCALE * 1.4426950408889634
BF = jnp.bfloat16
F32 = jnp.float32


def cost(flops, bytes_accessed, transcendentals=0):
    return pl.CostEstimate(flops=int(flops), bytes_accessed=int(bytes_accessed), transcendentals=int(transcendentals))


def whole(count):
    return [pl.BlockSpec(memory_space=pltpu.VMEM)] * count


def pack(arrays, widths, heads, step=4):
    rows = arrays[0].shape[0]
    total = sum(widths)

    def kernel(*refs):
        out = refs[-1]
        for j in range(step):
            at = 0
            for ref, w in zip(refs[:-1], widths):
                out[j, :, at : at + w] = ref[:, j * w : (j + 1) * w]
                at += w

    return pl.pallas_call(
        kernel,
        grid=(heads // step,),
        in_specs=[pl.BlockSpec((rows, step * w), lambda i: (0, i)) for w in widths],
        out_specs=pl.BlockSpec((step, rows, total), lambda i: (i, 0, 0)),
        out_shape=jax.ShapeDtypeStruct((heads, rows, total), arrays[0].dtype),
        cost_estimate=cost(0, 4 * heads * rows * total),
        name="pack",
    )(*arrays)


def unpack(packed, widths, step=4):
    heads, rows, total = packed.shape

    def kernel(*refs):
        src = refs[0]
        for j in range(step):
            at = 0
            for ref, w in zip(refs[1:], widths):
                ref[:, j * w : (j + 1) * w] = src[j, :, at : at + w]
                at += w

    return pl.pallas_call(
        kernel,
        grid=(heads // step,),
        in_specs=[pl.BlockSpec((step, rows, total), lambda i: (i, 0, 0))],
        out_specs=[pl.BlockSpec((rows, step * w), lambda i: (0, i)) for w in widths],
        out_shape=[jax.ShapeDtypeStruct((rows, heads * w), packed.dtype) for w in widths],
        cost_estimate=cost(0, 4 * heads * rows * total),
        name="unpack",
    )(packed)


def dot(a, b, ca, cb):
    return lax.dot_general(a, b, (((ca,), (cb,)), ((), ())), preferred_element_type=F32)


def fold(x, op):
    y = x[:, 0:D]
    for i in range(1, BLOCK // D):
        y = op(y, x[:, i * D : (i + 1) * D])
    return y


def attend(q, g, keys, values, old, hide):
    s = dot(q, keys, 1, 1)
    first = jnp.where(old, s[:, 0:BLOCK] if hide is None else s[:, 0:BLOCK] - hide[0], s[:, WINDOW:SPAN])
    parts = [first] + [s[:, c * BLOCK : (c + 1) * BLOCK] for c in range(1, CHUNKS)]
    top = fold(parts[0], jnp.maximum)
    for c in range(1, CHUNKS):
        y = fold(parts[c], jnp.maximum)
        top = jnp.maximum(top, y if hide is None else y - hide[c])
    top = jnp.max(top, axis=-1, keepdims=True) * RATE
    es = [jnp.exp2(parts[0] * RATE - top)]
    for c in range(1, CHUNKS):
        es.append(jnp.exp2(parts[c] * RATE - (top if hide is None else top + hide[c])))
    total = fold(es[0], jnp.add)
    for e in es[1:]:
        total = total + fold(e, jnp.add)
    inv = 1.0 / jnp.sum(total, axis=-1, keepdims=True)
    gf = g.astype(F32)
    gs = (gf * inv).astype(BF)
    eb = [e.astype(BF) for e in es]
    zero = jnp.zeros_like(eb[0])
    eb = jnp.concatenate([jnp.where(old, eb[0], zero)] + eb[1:] + [jnp.where(old, zero, eb[0])], axis=1)
    out = (dot(eb, values, 1, 0) * inv).astype(BF)
    delta = jnp.sum(gf * out.astype(F32), axis=-1, keepdims=True) * inv
    dp = dot(gs, values, 1, 1)
    dparts = [jnp.where(old, dp[:, 0:BLOCK], dp[:, WINDOW:SPAN])]
    dparts += [dp[:, c * BLOCK : (c + 1) * BLOCK] for c in range(1, CHUNKS)]
    ds = [(e * (x - delta)).astype(BF) for e, x in zip(es, dparts)]
    ds = jnp.concatenate([jnp.where(old, ds[0], zero)] + ds[1:] + [jnp.where(old, zero, ds[0])], axis=1)
    dq = (dot(ds, keys, 1, 0) * SCALE).astype(BF)
    return out, dq, (q, ds, gs, eb)


def attend_half(half, factor, qg, ka, a0, kb, b0, hide_when, acc_k, acc_v, put):
    row = lax.broadcasted_iota(jnp.int32, (BLOCK, BLOCK), 0)
    col = lax.broadcasted_iota(jnp.int32, (BLOCK, BLOCK), 1)
    old = col > row
    for b in range(CHUNKS):
        r = b * BLOCK
        rows = slice(half * WINDOW + r, half * WINDOW + r + BLOCK)
        ext = jnp.concatenate([ka[a0 + r : a0 + WINDOW, :], kb[b0 : b0 + r + BLOCK, :]], axis=0)
        keys, values = ext[:, 0:D], ext[:, D : 2 * D]
        hide = None
        if hide_when is not None:
            hide = [jnp.where(hide_when, 1e30, 0.0).astype(F32) if b + c < CHUNKS else 0.0 for c in range(CHUNKS)]
        saved = []
        for h in range(factor):
            q = qg[rows, h * D : (h + 1) * D]
            g = qg[rows, (factor + h) * D : (factor + h + 1) * D]
            out, dq, kept = attend(q, g, keys, values, old, hide)
            put(r, h, out, dq)
            saved.append(kept)
        dk = dot(*[jnp.concatenate([x[i] for x in saved], axis=0) for i in (0, 1)], 0, 0)
        dv = dot(*[jnp.concatenate([x[i] for x in saved], axis=0) for i in (2, 3)], 0, 0)
        seen = 0 if b == 0 else WINDOW
        for acc, part in ((acc_k, dk), (acc_v, dv)):
            if seen:
                acc[:, r : r + seen] += part[:, 0:seen]
            acc[:, r + seen : r + SPAN] = part[:, seen:SPAN]


def first_kernel(factor, lead_ref, qg, kv, halo, od, back, part, acc_k, acc_v):
    def put(r, h, out, dq):
        od[r : r + BLOCK, h * D : (h + 1) * D] = out
        od[r : r + BLOCK, (factor + h) * D : (factor + h + 1) * D] = dq

    attend_half(0, factor, qg, halo, 0, kv, 0, lead_ref[0] == 1, acc_k, acc_v, put)
    back[:, 0:D] = (acc_k[:, 0:WINDOW].T * SCALE).astype(BF)
    back[:, D : 2 * D] = acc_v[:, 0:WINDOW].T.astype(BF)
    part[:, 0:D] = acc_k[:, WINDOW : 2 * WINDOW].T
    part[:, D : 2 * D] = acc_v[:, WINDOW : 2 * WINDOW].T


def second_kernel(factor, qg, kv, od, part, out, last, acc_k, acc_v):
    width = 2 * factor * D
    out[0:WINDOW, 0:width] = od[...]

    def put(r, h, o, dq):
        out[WINDOW + r : WINDOW + r + BLOCK, h * D : (h + 1) * D] = o
        out[WINDOW + r : WINDOW + r + BLOCK, (factor + h) * D : (factor + h + 1) * D] = dq

    attend_half(1, factor, qg, kv, 0, kv, WINDOW, None, acc_k, acc_v, put)
    out[0:WINDOW, width : width + D] = ((acc_k[:, 0:WINDOW].T + part[:, 0:D]) * SCALE).astype(BF)
    out[0:WINDOW, width + D : width + 2 * D] = (acc_v[:, 0:WINDOW].T + part[:, D : 2 * D]).astype(BF)
    last[:, 0:D] = acc_k[:, WINDOW : 2 * WINDOW].T * SCALE
    last[:, D : 2 * D] = acc_v[:, WINDOW : 2 * WINDOW].T


def half_call(kernel, name, factor, out_shape, operands, scalars=0):
    pairs = factor * WINDOW * SPAN
    return pl.pallas_call(
        functools.partial(kernel, factor),
        in_specs=[pl.BlockSpec(memory_space=pltpu.SMEM)] * scalars + whole(len(operands) - scalars),
        out_specs=whole(len(out_shape)),
        out_shape=out_shape,
        scratch_shapes=[pltpu.VMEM((D, 2 * WINDOW), F32)] * 2,
        compiler_params=pltpu.CompilerParams(vmem_limit_bytes=40 * 1024 * 1024),
        cost_estimate=cost(12 * pairs * D, 8e6, pairs),
        name=name,
    )(*operands)


def body(queries, keys, values, output_cotangent):
    axes = ("row", "head")
    heads = lax.axis_size("row") * lax.axis_size("head")
    rows = queries.shape[0]
    wide = queries.shape[1] // heads
    slim = keys.shape[1] // heads
    factor = wide // D
    groups = lax.axis_size("group")
    tokens = heads * rows
    lead = (lax.axis_index("group") == 0).astype(jnp.int32).reshape(1)

    def spread(x):
        return lax.all_to_all(x, axes, split_axis=0, concat_axis=0, tiled=True)

    kv = spread(pack([keys, values], [slim, slim], heads)).reshape(tokens, 2 * slim)
    halo = lax.ppermute(kv[tokens - WINDOW :], "group", [(i, i + 1) for i in range(groups - 1)])
    qg = spread(pack([queries, output_cotangent], [wide, wide], heads)).reshape(tokens, 2 * wide)
    od, back, part = half_call(
        first_kernel,
        "attend_first",
        factor,
        [
            jax.ShapeDtypeStruct((WINDOW, 2 * wide), BF),
            jax.ShapeDtypeStruct((WINDOW, 2 * slim), BF),
            jax.ShapeDtypeStruct((WINDOW, 2 * slim), F32),
        ],
        [lead, qg, kv, halo],
        scalars=1,
    )
    more = lax.ppermute(back, "group", [(i + 1, i) for i in range(groups - 1)])
    out, last = half_call(
        second_kernel,
        "attend_second",
        factor,
        [jax.ShapeDtypeStruct((tokens, 2 * (wide + slim)), BF), jax.ShapeDtypeStruct((WINDOW, 2 * slim), F32)],
        [qg, kv, od, part],
    )
    out = out.at[WINDOW:, 2 * wide :].set((last + more.astype(F32)).astype(BF))
    out = spread(out.reshape(heads, rows, 2 * (wide + slim)))
    return unpack(out, [wide, wide, slim, slim])


def solution(mesh):
    row = 4
    seq, head = mesh.devices.shape
    finer = Mesh(mesh.devices.reshape(seq // row, row, head), ("group", "row", "head"))
    spec = P(("group", "row", "head"), None)
    return jax.shard_map(body, mesh=finer, in_specs=(spec,) * 4, out_specs=(spec,) * 4, check_vma=False)
```

time: 183 us -> 149 us (0.81)
  waiting for transfers between devices: 86 us -> 51.5 us
  blocking collectives: 21.8 us -> 44.3 us
  Pallas kernels: 44.3 us -> 31.8 us
  local copies, waits for them, and re-layouts: 4.77 us -> 0.83 us
  starting transfers between devices: 23.2 us -> 19.4 us
    all_to_all x3 -> x2, waiting for transfers between devices: 62.7 us -> 37.7 us  [spread(): return lax.all_to_all(x, axes, split_axis=0, concat_axis=0, tiled=True)]
    all_to_all x1, blocking collectives: 21.8 us -> 44.3 us  [spread(): return lax.all_to_all(x, axes, split_axis=0, concat_axis=0, tiled=True)]
    pallas_call x1 -> x2, Pallas kernels: 29.8 us -> 20.3 us  [half_call(): pl.pallas_call(functools.partial(kernel, factor), in_specs=[pl.BlockSpec(...]
    ppermute x1, waiting for transfers between devices: 12 us -> 3.25 us  [body(): more = lax.ppermute(back, 'group', [(i + 1, i) for i in range(groups - 1)])]
    all_to_all x3 -> x2, starting transfers between devices: 18.7 us -> 14 us  [spread(): return lax.all_to_all(x, axes, split_axis=0, concat_axis=0, tiled=True)]
    pallas_call x2 -> x1, Pallas kernels: 7.24 us -> 4.27 us  [unpack(): pl.pallas_call(kernel, grid=(heads // step,), in_specs=[pl.BlockSpec((ste...]
    unnamed x8 -> x0, local copies, waits for them, and re-layouts: 2.66 us -> none
  transfers between devices with their start and end apart: 5 -> 4, of which waited for: 5 -> 4; matrix products, arithmetic and copies ran while one was open for 1% -> 1% of each run, Pallas kernels for 4% -> 9%
where the time goes in v2:
time: 149 us
  waiting for transfers between devices  51.5 us (35%)
  blocking collectives  44.3 us (30%)
  Pallas kernels  31.8 us (21%)
  starting transfers between devices  19.4 us (13%)
    all_to_all x1, blocking collectives, spread(): return lax.all_to_all(x, axes, split_axis=0, concat_axis=0, tiled=True)  44.3 us
    all_to_all x2, waiting for transfers between devices, spread(): return lax.all_to_all(x, axes, split_axis=0, concat_axis=0, tiled=True)  37.7 us
    pallas_call x2, Pallas kernels, half_call(): pl.pallas_call(functools.partial(kernel, factor), in_specs=[pl.BlockSpec(...  20.3 us
    all_to_all x2, starting transfers between devices, spread(): return lax.all_to_all(x, axes, split_axis=0, concat_axis=0, tiled=True)  14 us
    ppermute x1, waiting for transfers between devices, body(): lax.ppermute(kv[tokens - WINDOW:], 'group', [(i, i + 1) for i in range(gr...  10.6 us
    pallas_call x2, Pallas kernels, pack(): pl.pallas_call(kernel, grid=(heads // step,), in_specs=[pl.BlockSpec((row...  7.23 us
    pallas_call x1, Pallas kernels, unpack(): pl.pallas_call(kernel, grid=(heads // step,), in_specs=[pl.BlockSpec((ste...  4.27 us
    ppermute x1, starting transfers between devices, body(): lax.ppermute(kv[tokens - WINDOW:], 'group', [(i, i + 1) for i in range(gr...  3.91 us
  transfers between devices with their start and end apart: 4, of which 4 were waited for; matrix products, arithmetic and copies ran while one was open for 1% of the time, Pallas kernels for 9%

profile of v2, /device:TPU:1, one launch (start us, length us, event | category | flops | bytes accessed | tf_op | source)
XLA Modules:
  0.0 148.5 jit_solution(7498023722552224163)
XLA Ops:
  0.6 3.5 %pack.3 = bf16[16,128,256]{2,1,0:T(8,128)(2,1)} custom-call(bf16[128,2048]{1,0:T(8,128)(2,1)} %refs_0_.3, bf16[128,2048]{1,0:T(8,128)(2,1)} %refs_1_.3), custom_call_target="tpu_custom_call" | custom-call | bytes 2097152 | tf_op jit(solution)/shard_map/pack/pallas_call | solution.py:41
  4.1 9.4 %all-to-all-start.1 = ((bf16[16,128,256]{2,1,0:T(8,128)(2,1)}), bf16[16,128,256]{2,1,0:T(8,128)(2,1)S(1)}, u32[]{:S(2)}, u32[]{:S(2)}) async-start(bf16[16,128,256]{2,1,0:T(8,128)(2,1)} %pack.3), calls=%async_computation.1 | async-start | bytes 2097152 | tf_op jit(solution)/shard_map/all_to_all | solution.py:198
  13.6 3.8 %pack.2 = bf16[16,128,512]{2,1,0:T(8,128)(2,1)} custom-call(bf16[128,4096]{1,0:T(8,128)(2,1)} %refs_0_.2, bf16[128,4096]{1,0:T(8,128)(2,1)} %refs_1_.2), custom_call_target="tpu_custom_call" | custom-call | bytes 4194304 | tf_op jit(solution)/shard_map/pack/pallas_call | solution.py:41
  17.3 13.3 %all-to-all-done.1 = bf16[16,128,256]{2,1,0:T(8,128)(2,1)S(1)} async-done(((bf16[16,128,256]{2,1,0:T(8,128)(2,1)}), bf16[16,128,256]{2,1,0:T(8,128)(2,1)S(1)}, u32[]{:S(2)}, u32[]{:S(2)}) %all-to-all-start.1) | async-done | bytes 1048608 | tf_op jit(solution)/shard_map/all_to_all | solution.py:198
  30.6 4.5 %all-to-all-start = ((bf16[16,128,512]{2,1,0:T(8,128)(2,1)}), bf16[16,128,512]{2,1,0:T(8,128)(2,1)S(1)}, u32[]{:S(2)}, u32[]{:S(2)}) async-start(bf16[16,128,512]{2,1,0:T(8,128)(2,1)} %pack.2), calls=%async_computation | async-start | bytes 4194304 | tf_op jit(solution)/shard_map/all_to_all | solution.py:198
  35.2 0.8 slice.31
  36.0 3.9 %collective-permute-start = (bf16[1024,256]{1,0:T(8,128)(2,1)}, bf16[1024,256]{1,0:T(8,128)(2,1)}, u32[]{:S(2)}, u32[]{:S(2)}) collective-permute-start(bf16[1024,256]{1,0:T(8,128)(2,1)} %bitcast.3), channel_id=1, source_target_pairs={{0,16},{16,32},{32,48},{48,64},{64,80},{80,96},{96,112},{1,17},{17... | collective-permute-start | bytes 1572872 | tf_op jit(solution)/shard_map/ppermute | solution.py:201
  39.9 10.6 %collective-permute-done.halo = bf16[1024,256]{1,0:T(8,128)(2,1)} collective-permute-done((bf16[1024,256]{1,0:T(8,128)(2,1)}, bf16[1024,256]{1,0:T(8,128)(2,1)}, u32[]{:S(2)}, u32[]{:S(2)}) %collective-permute-start) | collective-permute-done | bytes 524320 | tf_op jit(solution)/shard_map/ppermute | solution.py:201
  50.4 24.3 %all-to-all-done = bf16[16,128,512]{2,1,0:T(8,128)(2,1)S(1)} async-done(((bf16[16,128,512]{2,1,0:T(8,128)(2,1)}), bf16[16,128,512]{2,1,0:T(8,128)(2,1)S(1)}, u32[]{:S(2)}, u32[]{:S(2)}) %all-to-all-start) | async-done | bytes 2097184 | tf_op jit(solution)/shard_map/all_to_all | solution.py:198
  74.8 10.6 %attend_first.1 = (bf16[1024,512]{1,0:T(8,128)(2,1)S(1)}, bf16[1024,256]{1,0:T(8,128)(2,1)S(1)}, f32[1024,256]{1,0:T(8,128)S(1)}) custom-call(s32[1]{0:T(128)} %bitcast.2.lead_ref, bf16[2048,512]{1,0:T(8,128)(2,1)S(1)} %bitcast.8, bf16[2048,256]{1,0:T(8,128)(2,1)S(1)} %bitcast.6, bf16[1024,256]{1,0:T(8,128)(2,1)} %collective-permute-done.halo), custom_call_target="tpu_custom_call" | custom-call | flops 4026531840 | bytes 8000000 | tf_op jit(solution)/shard_map/attend_first/pallas_call | solution.py:174
  85.4 1.5 collective-permute-start.1
  86.9 9.7 %attend_second.1 = (bf16[2048,768]{1,0:T(8,128)(2,1)S(1)}, f32[1024,256]{1,0:T(8,128)S(1)}) custom-call(bf16[2048,512]{1,0:T(8,128)(2,1)S(1)} %bitcast.9, bf16[2048,256]{1,0:T(8,128)(2,1)S(1)} %bitcast.7, bf16[1024,512]{1,0:T(8,128)(2,1)S(1)} %get-tuple-element.21.od, f32[1024,256]{1,0:T(8,128)S(1)} %get-tuple-element.22.part), custom_call_target="tpu_custom_call" | custom-call | flops 4026531840 | bytes 8000000 | tf_op jit(solution)/shard_map/attend_second/pallas_call | solution.py:174
  96.6 3.2 %collective-permute-done.1 = bf16[1024,256]{1,0:T(8,128)(2,1)S(1)} collective-permute-done((bf16[1024,256]{1,0:T(8,128)(2,1)S(1)}, bf16[1024,256]{1,0:T(8,128)(2,1)S(1)}, u32[]{:S(2)}, u32[]{:S(2)}) %collective-permute-start.1) | collective-permute-done | bytes 524320 | tf_op jit(solution)/shard_map/ppermute | solution.py:215
  99.8 0.1 fusion
  99.9 44.3 %all_to_all.15.refs_0_ = bf16[16,128,768]{2,1,0:T(8,128)(2,1)} all-to-all(bf16[16,128,768]{2,1,0:T(8,128)(2,1)S(1)} %bitcast.5), channel_id=1, replica_groups=mesh['group'=8,'row'=4,'head'=4] {'row','head'}, dimensions={0} | all-to-all | bytes 6291456 | tf_op jit(solution)/shard_map/all_to_all | solution.py:198
  144.3 4.3 %unpack.1 = (bf16[128,4096]{1,0:T(8,128)(2,1)}, bf16[128,4096]{1,0:T(8,128)(2,1)}, bf16[128,2048]{1,0:T(8,128)(2,1)}, bf16[128,2048]{1,0:T(8,128)(2,1)}) custom-call(bf16[16,128,768]{2,1,0:T(8,128)(2,1)} %all_to_all.15.refs_0_), custom_call_target="tpu_custom_call" | custom-call | bytes 6291456 | tf_op jit(solution)/shard_map/unpack/pallas_call | solution.py:63
Async XLA Ops:
  4.1 26.5 %all-to-all-start.1 = ((bf16[16,128,256]{2,1,0:T(8,128)(2,1)}), bf16[16,128,256]{2,1,0:T(8,128)(2,1)S(1)}, u32[]{:S(2)}, u32[]{:S(2)}) async-start(bf16[16,128,256]{2,1,0:T(8,128)(2,1)} %pack.3), calls=%async_computation.1 | async-start | bytes 2097152 | tf_op jit(solution)/shard_map/all_to_all | solution.py:198
  30.6 44.2 %all-to-all-start = ((bf16[16,128,512]{2,1,0:T(8,128)(2,1)}), bf16[16,128,512]{2,1,0:T(8,128)(2,1)S(1)}, u32[]{:S(2)}, u32[]{:S(2)}) async-start(bf16[16,128,512]{2,1,0:T(8,128)(2,1)} %pack.2), calls=%async_computation | async-start | bytes 4194304 | tf_op jit(solution)/shard_map/all_to_all | solution.py:198
  36.0 14.5 %collective-permute-start = (bf16[1024,256]{1,0:T(8,128)(2,1)}, bf16[1024,256]{1,0:T(8,128)(2,1)}, u32[]{:S(2)}, u32[]{:S(2)}) collective-permute-start(bf16[1024,256]{1,0:T(8,128)(2,1)} %bitcast.3), channel_id=1, source_target_pairs={{0,16},{16,32},{32,48},{48,64},{64,80},{80,96},{96,112},{1,17},{17... | collective-permute-start | bytes 1572872 | tf_op jit(solution)/shard_map/ppermute | solution.py:201
  85.4 14.4 %collective-permute-start.1 = (bf16[1024,256]{1,0:T(8,128)(2,1)S(1)}, bf16[1024,256]{1,0:T(8,128)(2,1)S(1)}, u32[]{:S(2)}, u32[]{:S(2)}) collective-permute-start(bf16[1024,256]{1,0:T(8,128)(2,1)S(1)} %get-tuple-element.25), channel_id=1, source_target_pairs={{16,0},{32,16},{48,32},{64,48},{80,64},{96,80},{112,96},{17,1},{33... | collective-permute-start | bytes 1572872 | tf_op jit(solution)/shard_map/ppermute | solution.py:215

commit v3 on v2

--- a/solution.py
+++ b/solution.py
@@ -6,6 +6,7 @@
 from jax.experimental import pallas as pl
 from jax.experimental.pallas import tpu as pltpu
 from jax.sharding import Mesh, PartitionSpec as P
+
 
 D = 128
 WINDOW = 1024
@@ -26,46 +27,71 @@
     return [pl.BlockSpec(memory_space=pltpu.VMEM)] * count
 
 
-def pack(arrays, widths, heads, step=4):
-    rows = arrays[0].shape[0]
-    total = sum(widths)
+PIECES = 4
+
+
+def strips(widths, heads):
+    for j in range(heads):
+        at = 0
+        for i, w in enumerate(widths):
+            yield j, i, j * w, at, w
+            at += w
+
+
+def pack(arrays, widths, heads):
+    rows, total, n = arrays[0].shape[0], sum(widths), len(widths)
 
     def kernel(*refs):
-        out = refs[-1]
-        for j in range(step):
-            at = 0
-            for ref, w in zip(refs[:-1], widths):
-                out[j, :, at : at + w] = ref[:, j * w : (j + 1) * w]
-                at += w
+        src, out, held, sems = refs[:n], refs[n], refs[n + 1 : -1], refs[-1]
+        copies = []
+        for p in range(PIECES):
+            for i, w in enumerate(widths):
+                cols = pl.ds(p * w * heads // PIECES, w * heads // PIECES)
+                copies.append(pltpu.make_async_copy(src[i].at[:, cols], held[i].at[:, cols], sems.at[p * n + i]))
+        for copy in copies:
+            copy.start()
+        for j, i, there, here, w in strips(widths, heads):
+            if j % (heads // PIECES) == 0:
+                copies[j // (heads // PIECES) * n + i].wait()
+            out[j, :, here : here + w] = held[i][:, there : there + w]
 
     return pl.pallas_call(
         kernel,
-        grid=(heads // step,),
-        in_specs=[pl.BlockSpec((rows, step * w), lambda i: (0, i)) for w in widths],
-        out_specs=pl.BlockSpec((step, rows, total), lambda i: (i, 0, 0)),
+        in_specs=[pl.BlockSpec(memory_space=pltpu.HBM)] * n,
+        out_specs=pl.BlockSpec(memory_space=pltpu.VMEM),
         out_shape=jax.ShapeDtypeStruct((heads, rows, total), arrays[0].dtype),
+        scratch_shapes=[pltpu.VMEM(x.shape, x.dtype) for x in arrays] + [pltpu.SemaphoreType.DMA((PIECES * n,))],
         cost_estimate=cost(0, 4 * heads * rows * total),
         name="pack",
     )(*arrays)
 
 
-def unpack(packed, widths, step=4):
+def unpack(packed, widths):
     heads, rows, total = packed.shape
+    n = len(widths)
+    shapes = [jax.ShapeDtypeStruct((rows, heads * w), packed.dtype) for w in widths]
 
     def kernel(*refs):
-        src = refs[0]
-        for j in range(step):
-            at = 0
-            for ref, w in zip(refs[1:], widths):
-                ref[:, j * w : (j + 1) * w] = src[j, :, at : at + w]
-                at += w
+        src, out, held, sems = refs[0], refs[1 : 1 + n], refs[1 + n : -1], refs[-1]
+        copies = []
+        for j, i, there, here, w in strips(widths, heads):
+            held[i][:, there : there + w] = src[j, :, here : here + w]
+            p, last = divmod(j + 1, heads // PIECES)
+            if last == 0:
+                cols = pl.ds((p - 1) * w * heads // PIECES, w * heads // PIECES)
+                copy = pltpu.make_async_copy(held[i].at[:, cols], out[i].at[:, cols], sems.at[(p - 1) * n + i])
+                copy.start()
+                copies.append(copy)
+        for copy in copies:
+            copy.wait()
 
     return pl.pallas_call(
         kernel,
-        grid=(heads // step,),
-        in_specs=[pl.BlockSpec((step, rows, total), lambda i: (i, 0, 0))],
-        out_specs=[pl.BlockSpec((rows, step * w), lambda i: (0, i)) for w in widths],
-        out_shape=[jax.ShapeDtypeStruct((rows, heads * w), packed.dtype) for w in widths],
+        in_specs=[pl.BlockSpec(memory_space=pltpu.VMEM)],
+        out_specs=[pl.BlockSpec(memory_space=pl.ANY)] * n,
+        out_shape=shapes,
+        scratch_shapes=[pltpu.VMEM(x.shape, x.dtype) for x in shapes] + [pltpu.SemaphoreType.DMA((PIECES * n,))],
+        compiler_params=pltpu.CompilerParams(vmem_limit_bytes=16 * 1024 * 1024),
         cost_estimate=cost(0, 4 * heads * rows * total),
         name="unpack",
     )(packed)
@@ -142,19 +168,20 @@
             acc[:, r + seen : r + SPAN] = part[:, seen:SPAN]
 
 
-def first_kernel(factor, lead_ref, qg, kv, halo, od, back, part, acc_k, acc_v):
+def first_kernel(factor, lead_ref, data, halo, od, back, part, acc_k, acc_v):
     def put(r, h, out, dq):
         od[r : r + BLOCK, h * D : (h + 1) * D] = out
         od[r : r + BLOCK, (factor + h) * D : (factor + h + 1) * D] = dq
 
-    attend_half(0, factor, qg, halo, 0, kv, 0, lead_ref[0] == 1, acc_k, acc_v, put)
+    kv = data.at[:, 2 * factor * D :]
+    attend_half(0, factor, data, halo, 0, kv, 0, lead_ref[0] == 1, acc_k, acc_v, put)
     back[:, 0:D] = (acc_k[:, 0:WINDOW].T * SCALE).astype(BF)
     back[:, D : 2 * D] = acc_v[:, 0:WINDOW].T.astype(BF)
     part[:, 0:D] = acc_k[:, WINDOW : 2 * WINDOW].T
     part[:, D : 2 * D] = acc_v[:, WINDOW : 2 * WINDOW].T
 
 
-def second_kernel(factor, qg, kv, od, part, out, last, acc_k, acc_v):
+def second_kernel(factor, data, od, part, out, last, acc_k, acc_v):
     width = 2 * factor * D
     out[0:WINDOW, 0:width] = od[...]
 
@@ -162,14 +189,15 @@
         out[WINDOW + r : WINDOW + r + BLOCK, h * D : (h + 1) * D] = o
         out[WINDOW + r : WINDOW + r + BLOCK, (factor + h) * D : (factor + h + 1) * D] = dq
 
-    attend_half(1, factor, qg, kv, 0, kv, WINDOW, None, acc_k, acc_v, put)
+    kv = data.at[:, 2 * factor * D :]
+    attend_half(1, factor, data, kv, 0, kv, WINDOW, None, acc_k, acc_v, put)
     out[0:WINDOW, width : width + D] = ((acc_k[:, 0:WINDOW].T + part[:, 0:D]) * SCALE).astype(BF)
     out[0:WINDOW, width + D : width + 2 * D] = (acc_v[:, 0:WINDOW].T + part[:, D : 2 * D]).astype(BF)
     last[:, 0:D] = acc_k[:, WINDOW : 2 * WINDOW].T * SCALE
     last[:, D : 2 * D] = acc_v[:, WINDOW : 2 * WINDOW].T
 
 
-def half_call(kernel, name, factor, out_shape, operands, scalars=0):
+def half_call(kernel, factor, out_shape, operands, scalars=0):
     pairs = factor * WINDOW * SPAN
     return pl.pallas_call(
         functools.partial(kernel, factor),
@@ -177,9 +205,8 @@
         out_specs=whole(len(out_shape)),
         out_shape=out_shape,
         scratch_shapes=[pltpu.VMEM((D, 2 * WINDOW), F32)] * 2,
-        compiler_params=pltpu.CompilerParams(vmem_limit_bytes=40 * 1024 * 1024),
+        compiler_params=pltpu.CompilerParams(vmem_limit_bytes=20 * 1024 * 1024),
         cost_estimate=cost(12 * pairs * D, 8e6, pairs),
-        name=name,
     )(*operands)
 
 
@@ -197,28 +224,26 @@
     def spread(x):
         return lax.all_to_all(x, axes, split_axis=0, concat_axis=0, tiled=True)
 
-    kv = spread(pack([keys, values], [slim, slim], heads)).reshape(tokens, 2 * slim)
-    halo = lax.ppermute(kv[tokens - WINDOW :], "group", [(i, i + 1) for i in range(groups - 1)])
-    qg = spread(pack([queries, output_cotangent], [wide, wide], heads)).reshape(tokens, 2 * wide)
+    packed = pack([queries, output_cotangent, keys, values], [wide, wide, slim, slim], heads)
+    data = spread(packed).reshape(tokens, 2 * (wide + slim))
+    halo = lax.ppermute(data[tokens - WINDOW :, 2 * wide :], "group", [(i, i + 1) for i in range(groups - 1)])
     od, back, part = half_call(
         first_kernel,
-        "attend_first",
         factor,
         [
             jax.ShapeDtypeStruct((WINDOW, 2 * wide), BF),
             jax.ShapeDtypeStruct((WINDOW, 2 * slim), BF),
             jax.ShapeDtypeStruct((WINDOW, 2 * slim), F32),
         ],
-        [lead, qg, kv, halo],
+        [lead, data, halo],
         scalars=1,
     )
     more = lax.ppermute(back, "group", [(i + 1, i) for i in range(groups - 1)])
     out, last = half_call(
         second_kernel,
-        "attend_second",
         factor,
         [jax.ShapeDtypeStruct((tokens, 2 * (wide + slim)), BF), jax.ShapeDtypeStruct((WINDOW, 2 * slim), F32)],
-        [qg, kv, od, part],
+        [data, od, part],
     )
     out = out.at[WINDOW:, 2 * wide :].set((last + more.astype(F32)).astype(BF))
     out = spread(out.reshape(heads, rows, 2 * (wide + slim)))

time: 149 us -> 143 us (0.960); the launches traced: 149 us -> 141 us
  blocking collectives: 44.3 us -> 95 us
  waiting for transfers between devices: 51.5 us -> 12.6 us
  starting transfers between devices: 19.4 us -> 5.37 us
  Pallas kernels: 31.8 us -> 25.8 us
    all_to_all x1 -> x2, blocking collectives: 44.3 us -> 95 us  [spread(): return lax.all_to_all(x, axes, split_axis=0, concat_axis=0, tiled=True)]
    all_to_all x2 -> x0, waiting for transfers between devices: 37.7 us -> none  [spread(): return lax.all_to_all(x, axes, split_axis=0, concat_axis=0, tiled=True)]
    all_to_all x2 -> x0, starting transfers between devices: 14 us -> none  [spread(): return lax.all_to_all(x, axes, split_axis=0, concat_axis=0, tiled=True)]
    pallas_call x3 -> x2, Pallas kernels: 11.5 us -> 5.52 us  [the longest x1 3.69 us: pack(): pl.pallas_call(kernel, in_specs=[pl.BlockSpec(memory_space=pltpu.HBM)] *...]
  transfers between devices with their start and end apart: 4 -> 2, of which waited for: 4 -> 2; matrix products, arithmetic and copies ran while one was open for 1% -> 0% of each run, Pallas kernels for 9% -> 7%
where the time goes in v3:
time: 143 us; the launch traced here: 141 us
  blocking collectives  95 us (66%)
  Pallas kernels  25.8 us (18%)
  waiting for transfers between devices  12.6 us (9%)
  starting transfers between devices  5.37 us (4%)
    all_to_all x2, blocking collectives, spread(): return lax.all_to_all(x, axes, split_axis=0, concat_axis=0, tiled=True)  95 us
    pallas_call x2, Pallas kernels, half_call(): pl.pallas_call(functools.partial(kernel, factor), in_specs=[pl.BlockSpec(...  20.3 us
    ppermute x1, waiting for transfers between devices, body(): lax.ppermute(data[tokens - WINDOW:, 2 * wide:], 'group', [(i, i + 1) for...  9.52 us
    ppermute x1, starting transfers between devices, body(): lax.ppermute(data[tokens - WINDOW:, 2 * wide:], 'group', [(i, i + 1) for...  3.9 us
    pallas_call x1, Pallas kernels, pack(): pl.pallas_call(kernel, in_specs=[pl.BlockSpec(memory_space=pltpu.HBM)] *...  3.69 us
    ppermute x1, waiting for transfers between devices, body(): more = lax.ppermute(back, 'group', [(i + 1, i) for i in range(groups - 1)])  3.12 us
  transfers between devices with their start and end apart: 2, of which 2 were waited for; matrix products, arithmetic and copies ran while one was open for 0% of the time, Pallas kernels for 7%

profile of v3, /device:TPU:1, one launch (start us, length us, event | category | flops | bytes accessed | tf_op | source)
XLA Modules:
  0.0 140.5 jit_solution(5017986971070453734)
XLA Ops:
  0.6 3.7 %pack.1 = bf16[16,128,768]{2,1,0:T(8,128)(2,1)} custom-call(bf16[128,4096]{1,0:T(8,128)(2,1)} %refs_0_.1, bf16[128,4096]{1,0:T(8,128)(2,1)} %refs_1_.1, bf16[128,2048]{1,0:T(8,128)(2,1)} %refs_2_.1, bf16[128,2048]{1,0:T(8,128)(2,1)} %refs_3_.1), custom_call_target="tpu_custom_call" | custom-call | bytes 6291456 | tf_op jit(solution)/shard_map/pack/pallas_call | solution.py:58
  4.3 48.7 %all_to_all.10 = bf16[16,128,768]{2,1,0:T(8,128)(2,1)S(1)} all-to-all(bf16[16,128,768]{2,1,0:T(8,128)(2,1)} %pack.1), channel_id=1, replica_groups=mesh['group'=8,'row'=4,'head'=4] {'row','head'}, dimensions={0} | all-to-all | bytes 6291456 | tf_op jit(solution)/shard_map/all_to_all | solution.py:225
  53.0 0.8 slice.27
  53.9 3.9 %collective-permute-start = (bf16[1024,256]{1,0:T(8,128)(2,1)}, bf16[1024,256]{1,0:T(8,128)(2,1)}, u32[]{:S(2)}, u32[]{:S(2)}) collective-permute-start(bf16[1024,256]{1,0:T(8,128)(2,1)} %slice.27), channel_id=1, source_target_pairs={{0,16},{16,32},{32,48},{48,64},{64,80},{80,96},{96,112},{1,17},{17... | collective-permute-start | bytes 1572872 | tf_op jit(solution)/shard_map/ppermute | solution.py:229
  57.8 9.5 %collective-permute-done.halo = bf16[1024,256]{1,0:T(8,128)(2,1)} collective-permute-done((bf16[1024,256]{1,0:T(8,128)(2,1)}, bf16[1024,256]{1,0:T(8,128)(2,1)}, u32[]{:S(2)}, u32[]{:S(2)}) %collective-permute-start) | collective-permute-done | bytes 524320 | tf_op jit(solution)/shard_map/ppermute | solution.py:229
  67.3 10.6 %shard_map.75 = (bf16[1024,512]{1,0:T(8,128)(2,1)S(1)}, bf16[1024,256]{1,0:T(8,128)(2,1)S(1)}, f32[1024,256]{1,0:T(8,128)S(1)}) custom-call(s32[1]{0:T(128)} %bitcast.1.lead_ref, bf16[2048,768]{1,0:T(8,128)(2,1)S(1)} %bitcast.4, bf16[1024,256]{1,0:T(8,128)(2,1)} %collective-permute-done.halo), custom_call_target="tpu_custom_call" | custom-call | flops 4026531840 | bytes 8000000 | tf_op jit(solution)/shard_map/pallas_call | solution.py:202
  77.9 1.5 %collective-permute-start.1 = (bf16[1024,256]{1,0:T(8,128)(2,1)S(1)}, bf16[1024,256]{1,0:T(8,128)(2,1)S(1)}, u32[]{:S(2)}, u32[]{:S(2)}) collective-permute-start(bf16[1024,256]{1,0:T(8,128)(2,1)S(1)} %get-tuple-element.25), channel_id=1, source_target_pairs={{16,0},{32,16},{48,32},{64,48},{80,64},{96,80},{112,96},{17,1},{33... | collective-permute-start | bytes 1572872 | tf_op jit(solution)/shard_map/ppermute | solution.py:241
  79.4 9.7 %shard_map.76 = (bf16[2048,768]{1,0:T(8,128)(2,1)S(1)}, f32[1024,256]{1,0:T(8,128)S(1)}) custom-call(bf16[2048,768]{1,0:T(8,128)(2,1)S(1)} %bitcast.5, bf16[1024,512]{1,0:T(8,128)(2,1)S(1)} %get-tuple-element.21.od, f32[1024,256]{1,0:T(8,128)S(1)} %get-tuple-element.22.part), custom_call_target="tpu_custom_call" | custom-call | flops 4026531840 | bytes 8000000 | tf_op jit(solution)/shard_map/pallas_call | solution.py:202
  89.1 3.1 %collective-permute-done.1 = bf16[1024,256]{1,0:T(8,128)(2,1)S(1)} collective-permute-done((bf16[1024,256]{1,0:T(8,128)(2,1)S(1)}, bf16[1024,256]{1,0:T(8,128)(2,1)S(1)}, u32[]{:S(2)}, u32[]{:S(2)}) %collective-permute-start.1) | collective-permute-done | bytes 524320 | tf_op jit(solution)/shard_map/ppermute | solution.py:241
  92.2 0.1 fusion
  92.3 46.3 %all_to_all.11.refs_0_ = bf16[16,128,768]{2,1,0:T(8,128)(2,1)S(1)} all-to-all(bf16[16,128,768]{2,1,0:T(8,128)(2,1)S(1)} %bitcast.6), channel_id=1, replica_groups=mesh['group'=8,'row'=4,'head'=4] {'row','head'}, dimensions={0} | all-to-all | bytes 6291456 | tf_op jit(solution)/shard_map/all_to_all | solution.py:225
  138.5 1.8 %unpack.1 = (bf16[128,4096]{1,0:T(8,128)(2,1)}, bf16[128,4096]{1,0:T(8,128)(2,1)}, bf16[128,2048]{1,0:T(8,128)(2,1)}, bf16[128,2048]{1,0:T(8,128)(2,1)}) custom-call(bf16[16,128,768]{2,1,0:T(8,128)(2,1)S(1)} %all_to_all.11.refs_0_), custom_call_target="tpu_custom_call" | custom-call | bytes 6291456 | tf_op jit(solution)/shard_map/unpack/pallas_call | solution.py:88
Async XLA Ops:
  53.9 13.4 %collective-permute-start = (bf16[1024,256]{1,0:T(8,128)(2,1)}, bf16[1024,256]{1,0:T(8,128)(2,1)}, u32[]{:S(2)}, u32[]{:S(2)}) collective-permute-start(bf16[1024,256]{1,0:T(8,128)(2,1)} %slice.27), channel_id=1, source_target_pairs={{0,16},{16,32},{32,48},{48,64},{64,80},{80,96},{96,112},{1,17},{17... | collective-permute-start | bytes 1572872 | tf_op jit(solution)/shard_map/ppermute | solution.py:229
  77.9 14.3 %collective-permute-start.1 = (bf16[1024,256]{1,0:T(8,128)(2,1)S(1)}, bf16[1024,256]{1,0:T(8,128)(2,1)S(1)}, u32[]{:S(2)}, u32[]{:S(2)}) collective-permute-start(bf16[1024,256]{1,0:T(8,128)(2,1)S(1)} %get-tuple-element.25), channel_id=1, source_target_pairs={{16,0},{32,16},{48,32},{64,48},{80,64},{96,80},{112,96},{17,1},{33... | collective-permute-start | bytes 1572872 | tf_op jit(solution)/shard_map/ppermute | solution.py:241
